TPU v7x, 32 devices: a whole 2x2x4 slice. The times are simulated.
32 devices in a mesh: blocks: 8 (over y, x, core), slab: 4 (over z).
Axes of the slice: x: 2, y: 2, z: 4, core: 2. Of those that a mesh axis runs over, the one named last changes fastest.
Arguments:
- populations: float32 [19, 4, 8, 4096], P(None, 'slab', 'blocks'), may hold values from -6 to 6
- w_in: bfloat16 [512, 19], replicated, may hold values from -1.25 to 1.25
- w_mid: bfloat16 [1, 512, 512], replicated, may hold values from -0.25 to 0.25
- w_out: bfloat16 [19, 512], replicated, may hold values from -0.25 to 0.25
- cotangent: float32 [19, 4, 8, 4096], P(None, 'slab', 'blocks'), may hold values from -6 to 6
- face_source: int32 [8, 4], replicated, may hold values from 0 to 7, as said below
- face_level: int32 [4, 8, 6], P('slab', 'blocks'), may hold values 0 or 1
- face_quadrant: int32 [4, 8, 6], P('slab', 'blocks'), may hold values from 0 to 3
Outputs:
- final: float32 [19, 4, 8, 4096], P(None, 'slab', 'blocks')
- grad_pops: float32 [19, 4, 8, 4096], P(None, 'slab', 'blocks')
- grad_in: float32 [512, 19], replicated
- grad_mid: float32 [1, 512, 512], replicated
- grad_out: float32 [19, 512], replicated
Inputs may be any that keep to these rules, and one draw needn't show every extreme that they name: face_source is symmetric: face_source[face_source[b, f], f xor 1] = b. The +y and -y neighbours of block b are the same block, b xor 1. Every neighbour's index differs from the block's by at most 3 modulo 8, never by 0, and that distance is reached.
All inputs are finite; a program needn't handle non-finite values. No bound on the sum of `face_level` on one device may be relied on, other than what follows from the above.
Results may differ from a plain program's by a relative error of at most 0.0088.
Values sent between devices are 32-bit elements; how exact they have to be, the bound alone decides.
A program may use at most 128 MiB of HBM per device.

v0:
```python
import functools

import jax
import jax.numpy as jnp
import numpy as np
from jax import lax
from jax.experimental import pallas as pl
from jax.experimental.pallas import tpu as pltpu
from jax.sharding import PartitionSpec as P

REACH = 3
R = 24
S = 16
A = S * S
CHUNK = 1024
MESH = pl.DeviceIdType.MESH
F32, BF16 = jnp.float32, jnp.bfloat16

VELOCITIES = [
    (0, 0, 0),
    (1, 0, 0),
    (-1, 0, 0),
    (0, 1, 0),
    (0, -1, 0),
    (0, 0, 1),
    (0, 0, -1),
    (1, 1, 0),
    (-1, -1, 0),
    (1, -1, 0),
    (-1, 1, 0),
    (1, 0, 1),
    (-1, 0, -1),
    (1, 0, -1),
    (-1, 0, 1),
    (0, 1, 1),
    (0, -1, -1),
    (0, 1, -1),
    (0, -1, 1),
]
Q = len(VELOCITIES)


def row_table():
    table = np.zeros((4, R, A), np.int32)
    for q, v in enumerate(VELOCITIES):
        for axis in range(3):
            table[axis, q] = v[axis]
        if q:
            table[3, q] = 1 if q % 2 else -1
    return table


def lane_roll(x, shift):
    shift %= A
    return x if shift == 0 else pltpu.roll(x, shift, 1)


class Geometry:
    def __init__(self, table_ref):
        lane = lax.broadcasted_iota(jnp.int32, (R, A), 1)
        y, z = lane // S, lane % S
        self.v = [table_ref[axis] for axis in range(3)]
        self.plus = [v == 1 for v in self.v]
        self.minus = [v == -1 for v in self.v]
        parity = table_ref[3]
        self.odd, self.even = parity == 1, parity == -1
        py, my, pz, mz = self.plus[1], self.minus[1], self.plus[2], self.minus[2]
        self.ly = (py & (y == 0)) | (my & (y == S - 1))
        self.lz = (pz & (z == 0)) | (mz & (z == S - 1))
        self.oy = (py & (y == S - 1)) | (my & (y == 0))
        self.oz = (pz & (z == S - 1)) | (mz & (z == 0))

    def row_roll(self, x, axis, step, sign=1):
        up, down = lane_roll(x, sign * step), lane_roll(x, -sign * step)
        return jnp.where(self.plus[axis], up, jnp.where(self.minus[axis], down, x))

    def opposite(self, x):
        return jnp.where(self.odd, pltpu.roll(x, R - 1, 0), jnp.where(self.even, pltpu.roll(x, 1, 0), x))

    def leaving_x(self, k):
        if k == 0:
            return self.plus[0]
        if k == S - 1:
            return self.minus[0]
        return None

    def crossings(self, k):
        ly, lz, lx = self.ly, self.lz, self.leaving_x(k)
        two, some = ly & lz, ly | lz
        if lx is None:
            return ly & ~lz, lz & ~ly, None, two, ~some
        return (
            ly & ~lz & ~lx,
            lz & ~ly & ~lx,
            lx & ~some,
            two | (lx & some),
            ~(some | lx),
        )


def layer(ref, k):
    return ref[:, k * A : (k + 1) * A]


def put(ref, k, value):
    ref[:, k * A : (k + 1) * A] = value


def split3(x):
    hi = x.astype(BF16)
    rest = x - hi.astype(F32)
    mid = rest.astype(BF16)
    low = (rest - mid.astype(F32)).astype(BF16)
    return jnp.concatenate([hi, mid, low], axis=0)


def refine(g, sheet, axis, pick_ref, transposed):
    parts = split3(sheet)
    dims = (((1,), (1 if transposed else 0,)), ((), ()))
    both = []
    for face in (2 * axis, 2 * axis + 1):
        r = lax.dot_general(parts, pick_ref[face], dims, preferred_element_type=F32)
        both.append(r[:R] + r[R : 2 * R] + r[2 * R :])
    return jnp.where(g.minus[axis], both[0], both[1])


PACK = [
    [(0, 1, 3), (2, 7, 15)],
    [(0, 3, 5), (2, 7, 11), (6, 15, 19)],
    [(0, 5, 7), (2, 11, 19)],
]
FACED = 10


def pack(sheets_ref, axis, base, value):
    for at, low, high in PACK[axis]:
        sheets_ref[axis, base + at : base + at + high - low] = value[low:high]


def unpack(recv_ref, slot, axis, base, tmp_ref):
    tmp_ref[...] = jnp.zeros(tmp_ref.shape, F32)
    for at, low, high in PACK[axis]:
        tmp_ref[low:high] = recv_ref[slot, base + at : base + at + high - low]
    return tmp_ref[...]


def slot_of(source_ref, blocks, face):
    me = lax.axis_index("blocks")
    distance = lax.rem(source_ref[face, me] - me + blocks, blocks)
    distance = jnp.where(distance > blocks // 2, distance - blocks, distance)
    slot = jnp.where(distance < 0, distance + REACH, distance + REACH - 1)
    return jnp.clip(slot, 0, 2 * REACH - 1)


def gather_sheets(g, ref, sheets_ref):
    acc_y = acc_z = None
    for k in range(S):
        a = layer(ref, k)
        ty = lane_roll(jnp.where(g.oy, a, 0.0), S * k)
        tz = lane_roll(jnp.where(g.oz, a, 0.0), k)
        acc_y = ty if acc_y is None else acc_y + ty
        acc_z = tz if acc_z is None else acc_z + tz
    sheet_x = jnp.where(g.plus[0], layer(ref, S - 1), jnp.where(g.minus[0], layer(ref, 0), 0.0))
    pack(sheets_ref, 0, 0, sheet_x)
    pack(sheets_ref, 1, 0, jnp.where(g.plus[1], lane_roll(acc_y, S), acc_y))
    pack(sheets_ref, 2, 0, jnp.where(g.plus[2], lane_roll(acc_z, -(S - 1)), acc_z))


def gather_bars(g, ref, pick_ref, sheets_ref):
    acc_x = acc_y = acc_z = None
    for k in range(S):
        b = layer(ref, k)
        one_y, one_z, one_x, _, _ = g.crossings(k)
        ty = lane_roll(jnp.where(one_y, b, 0.0), S * k)
        tz = lane_roll(jnp.where(one_z, b, 0.0), k)
        acc_y = ty if acc_y is None else acc_y + ty
        acc_z = tz if acc_z is None else acc_z + tz
        if one_x is not None:
            tx = jnp.where(one_x, b, 0.0)
            acc_x = tx if acc_x is None else acc_x + tx
    acc_y = jnp.where(g.minus[1], lane_roll(acc_y, S), acc_y)
    acc_z = jnp.where(g.minus[2], lane_roll(acc_z, -(S - 1)), acc_z)
    gx = g.row_roll(g.row_roll(acc_x, 1, S, -1), 2, 1, -1)
    gy = g.row_roll(g.row_roll(acc_y, 0, S, -1), 2, 1, -1)
    gz = g.row_roll(g.row_roll(acc_z, 1, S, -1), 0, 1, -1)
    for axis, value in enumerate((gx, gy, gz)):
        pack(sheets_ref, axis, FACED, refine(g, value, axis, pick_ref, True))


def received(g, recv_ref, slots, base, toward, tmp_ref):
    sides = [unpack(recv_ref, slot, 0, base, tmp_ref) for slot in slots]
    x = jnp.where(toward[0], sides[0], sides[1])
    y = unpack(recv_ref, 2 * REACH, 1, base, tmp_ref)
    sides = [unpack(recv_ref, 2 * REACH + side, 2, base, tmp_ref) for side in (1, 2)]
    return x, y, jnp.where(toward[2], sides[0], sides[1])


def stream(g, post_ref, recv_ref, slots, pick_ref, tmp_ref, store):
    raw_x, raw_y, raw_z = received(g, recv_ref, slots, 0, g.minus, tmp_ref)
    gx, gy, gz = (refine(g, raw, axis, pick_ref, False) for axis, raw in enumerate((raw_x, raw_y, raw_z)))
    sx = g.row_roll(g.row_roll(gx, 1, S), 2, 1)
    sy = g.row_roll(g.row_roll(gy, 0, S), 2, 1)
    sz = g.row_roll(g.row_roll(gz, 1, S), 0, 1)
    sy = jnp.where(g.minus[1], lane_roll(sy, -S), sy)
    sz = jnp.where(g.minus[2], lane_roll(sz, S - 1), sz)
    for k in range(S):
        here = layer(post_ref, k)
        behind = layer(post_ref, max(k - 1, 0))
        ahead = layer(post_ref, min(k + 1, S - 1))
        moved = jnp.where(g.plus[0], behind, jnp.where(g.minus[0], ahead, here))
        moved = g.row_roll(g.row_roll(moved, 1, S), 2, 1)
        one_y, one_z, one_x, two, _ = g.crossings(k)
        out = jnp.where(one_y, lane_roll(sy, -S * k), moved)
        out = jnp.where(one_z, lane_roll(sz, -k), out)
        if one_x is not None:
            out = jnp.where(one_x, sx, out)
        out = jnp.where(two, g.opposite(here), out)
        store(k, out)


def stream_back(g, bar_ref, recv_ref, slots, tmp_ref, work_ref, out_ref):
    ox, oy, oz = received(g, recv_ref, slots, FACED, g.plus, tmp_ref)
    oy = jnp.where(g.plus[1], lane_roll(oy, -S), oy)
    oz = jnp.where(g.plus[2], lane_roll(oz, S - 1), oz)
    for k in range(S):
        put(work_ref, k, jnp.where(g.crossings(k)[4], layer(bar_ref, k), 0.0))
    for k in range(S):
        zero = jnp.zeros((R, A), F32)
        ahead = layer(work_ref, k + 1) if k + 1 < S else zero
        behind = layer(work_ref, k - 1) if k > 0 else zero
        moved = jnp.where(g.plus[0], ahead, jnp.where(g.minus[0], behind, layer(work_ref, k)))
        out = g.row_roll(g.row_roll(moved, 1, S, -1), 2, 1, -1)
        out += g.opposite(jnp.where(g.crossings(k)[3], layer(bar_ref, k), 0.0))
        out += jnp.where(g.oy, lane_roll(oy, -S * k), 0.0)
        out += jnp.where(g.oz, lane_roll(oz, -k), 0.0)
        if k == 0:
            out += jnp.where(g.minus[0], ox, 0.0)
        if k == S - 1:
            out += jnp.where(g.plus[0], ox, 0.0)
        put(out_ref, k, out)


def mm(a, b):
    return jnp.dot(a, b, preferred_element_type=F32)


def outer(a, b):
    return lax.dot_general(a, b, (((1,), (1,)), ((), ())), preferred_element_type=F32)


def slope(h):
    wide = h.astype(F32)
    return 1.0 - wide * wide


def collide(x, w_in, w_mid, w_out):
    inputs = x.astype(BF16)
    h0 = jnp.tanh(mm(w_in[...], inputs)).astype(BF16)
    h1 = jnp.tanh(mm(w_mid[...], h0)).astype(BF16)
    return inputs, h0, h1, x + mm(w_out[...], h1)


def collide_back(bar, inputs, h0, h1, w_in_t, w_mid_t, w_out_t, grads_ref, hid):
    e = bar.astype(BF16)
    a1 = (mm(w_out_t[...], e) * slope(h1)).astype(BF16)
    a0 = (mm(w_mid_t[...], a1) * slope(h0)).astype(BF16)
    grads_ref[:hid] += outer(a1, h0)
    grads_ref[hid : hid + R] += outer(inputs, a0)
    grads_ref[hid + R : hid + 2 * R] += outer(e, h1)
    return bar + mm(w_in_t[...], a0)


def span(i):
    return pl.ds(pl.multiple_of(i * CHUNK, CHUNK), CHUNK)


LANES = 128


def load_rows(dst, src):
    lines = dst.shape[1] // LANES
    dst[16:] = jnp.zeros((R - 16, dst.shape[1]), F32)
    for i in range(lines):
        dst[:Q, i * LANES : (i + 1) * LANES] = src[pl.ds(i, Q, stride=lines), :]


def store_lines(dst, first, value):
    lines = dst.shape[0] // Q
    for i in range(value.shape[1] // LANES):
        dst[pl.ds(first + i, Q, stride=lines), :] = value[:Q, i * LANES : (i + 1) * LANES]


def one_hot_layers(level, quadrant, pick):
    half = S // 2
    target = lax.broadcasted_iota(jnp.int32, (A, A), 1)
    source = lax.broadcasted_iota(jnp.int32, (A, A), 0)
    row, col = target // S, target % S
    fine = row // 2 * S + col // 2
    for face in range(6):
        q = quadrant[0, 0, face]
        high, low = q // 2, q % 2
        if face >= 4:
            high, low = low, high
        corner = high * half * S + low * half
        wanted = jnp.where(level[0, 0, face] == 1, corner + fine, target)
        pick[face] = jnp.where(source == wanted, 1.0, 0.0).astype(BF16)


def padded_rows(src, tall, flat, flipped):
    tall[...] = jnp.zeros(tall.shape, F32)
    tall[:Q] = src[...].astype(F32)
    flat[...] = tall[...].astype(BF16)
    flipped[...] = tall[...].T.astype(BF16)


def first_kernel(
    level, quadrant, table, pops, cot, w_in_rows, w_mid, w_out_rows,
    post, h_hbm, sheets, pick, w_in, w_in_t, w_out, w_out_t, w_mid_t, wide, cot_wide, h_buf, tall, sems,
):
    g = Geometry(table)
    cells = wide.shape[1]
    load_rows(wide, pops)
    load_rows(cot_wide, cot)
    padded_rows(w_in_rows, tall, w_in_t, w_in)
    padded_rows(w_out_rows, tall, w_out, w_out_t)
    w_mid_t[...] = w_mid[...].astype(F32).T.astype(BF16)
    one_hot_layers(level, quadrant, pick)
    sheets[...] = jnp.zeros(sheets.shape, F32)

    def moved(i, j):
        return pltpu.make_async_copy(h_buf.at[j, :, span(i)], h_hbm.at[j, :, span(i)], sems.at[j, i])

    @pl.loop(0, cells // CHUNK)
    def _(i):
        at = span(i)
        _, h0, h1, out = collide(wide[:, at], w_in, w_mid, w_out)
        post[:, at] = out
        h_buf[0, :, at] = h0
        h_buf[1, :, at] = h1
        moved(i, 0).start()
        moved(i, 1).start()

    gather_sheets(g, post, sheets)
    gather_bars(g, cot_wide, pick, sheets)

    @pl.loop(0, cells // CHUNK)
    def _(i):
        moved(i, 0).wait()
        moved(i, 1).wait()


def middle_kernel(
    blocks, source, table, pick, recv, post1, cot, w_in, w_mid, w_out, w_in_t, w_mid_t, w_out_t,
    post2, bar, sheets, grads, state, wide, work, pbar, tmp,
):
    g = Geometry(table)
    cells = post1.shape[1]
    hid = w_mid.shape[0]
    slots = [slot_of(source, blocks, face) for face in (0, 1)]
    load_rows(wide, cot)
    stream(g, post1, recv, slots, pick, tmp, functools.partial(put, state))
    stream_back(g, wide, recv, slots, tmp, work, pbar)
    grads[...] = jnp.zeros(grads.shape, F32)
    sheets[...] = jnp.zeros(sheets.shape, F32)

    @pl.loop(0, cells // CHUNK)
    def _(i):
        at = span(i)
        inputs, h0, h1, out = collide(state[:, at], w_in, w_mid, w_out)
        post2[:, at] = out
        bar[:, at] = collide_back(pbar[:, at], inputs, h0, h1, w_in_t, w_mid_t, w_out_t, grads, hid)

    gather_sheets(g, post2, sheets)
    gather_bars(g, bar, pick, sheets)


def last_kernel(
    blocks, source, table, pick, recv, post2, bar, pops, h_hbm, grads_in, w_in_t, w_mid_t, w_out_t,
    final, grad_pops, grads, wide, work, pbar, tmp, h_buf, sems,
):
    g = Geometry(table)
    cells = post2.shape[1]
    hid = w_mid_t.shape[0]

    def moved(i, j):
        return pltpu.make_async_copy(h_hbm.at[j, :, span(i)], h_buf.at[j, :, span(i)], sems.at[j, i])

    @pl.loop(0, cells // CHUNK)
    def _(i):
        moved(i, 0).start()
        moved(i, 1).start()

    slots = [slot_of(source, blocks, face) for face in (0, 1)]
    load_rows(wide, pops)
    stream(g, post2, recv, slots, pick, tmp, lambda k, value: store_lines(final, k * A // LANES, value))
    stream_back(g, bar, recv, slots, tmp, work, pbar)
    grads[...] = grads_in[...]

    @pl.loop(0, cells // CHUNK)
    def _(i):
        at = span(i)
        moved(i, 0).wait()
        moved(i, 1).wait()
        out = collide_back(
            pbar[:, at], wide[:, at].astype(BF16), h_buf[0, :, at], h_buf[1, :, at],
            w_in_t, w_mid_t, w_out_t, grads, hid,
        )
        pbar[:, at] = out

    store_lines(grad_pops, 0, pbar[...])


OFFSETS = [d for d in range(-REACH, REACH + 1) if d != 0]


def exchange_kernel(blocks, slabs, sheets, recv, send_sem, recv_sem):
    me, level = lax.axis_index("blocks"), lax.axis_index("slab")
    side = [lax.rem(me - d + blocks, blocks) for d in OFFSETS]
    other = me + 1 - 2 * lax.rem(me, 2)
    above, below = lax.rem(level + 1, slabs), lax.rem(level + slabs - 1, slabs)
    barrier = pltpu.get_barrier_semaphore()
    for target in side:
        pl.semaphore_signal(barrier, inc=1, device_id={"blocks": target}, device_id_type=MESH)
    for target in (above, below):
        pl.semaphore_signal(barrier, inc=1, device_id={"slab": target}, device_id_type=MESH)
    pl.semaphore_wait(barrier, len(side) + 2)
    plan = [(0, i, {"blocks": target}) for i, target in enumerate(side)]
    plan.append((1, len(side), {"blocks": other}))
    plan.append((2, len(side) + 1, {"slab": below}))
    plan.append((2, len(side) + 2, {"slab": above}))
    copies = []
    for which, slot, device in plan:
        copy = pltpu.make_async_remote_copy(
            src_ref=sheets.at[which], dst_ref=recv.at[slot],
            send_sem=send_sem.at[slot], recv_sem=recv_sem.at[slot],
            device_id=device, device_id_type=MESH,
        )
        copy.start()
        copies.append(copy)
    for copy in copies:
        copy.wait()


PIECES = 3


def sum_kernel(chips, slabs, grads, out, land_c, half, land_t, part, land_s, sems):
    me, level = lax.axis_index("blocks"), lax.axis_index("slab")
    core, chip = lax.rem(me, 2), me // 2
    rows, width = part.shape[1], land_s.shape[-1]
    peer_t = [lax.rem(chip + d, chips) for d in range(1, chips)]
    peer_s = [lax.rem(level + d, slabs) for d in range(1, slabs)]
    twin = {"blocks": me + 1 - 2 * core}
    sides = [{"blocks": 2 * t + core} for t in peer_t]
    stack = [{"slab": t} for t in peer_s]
    barrier = pltpu.get_barrier_semaphore()
    for device in [twin] + sides + stack:
        pl.semaphore_signal(barrier, inc=1, device_id=device, device_id_type=MESH)
    pl.semaphore_wait(barrier, 1 + len(sides) + len(stack))

    def send(src, dst, p, which, device):
        copy = pltpu.make_async_remote_copy(
            src_ref=src, dst_ref=dst, send_sem=sems.at[0, p, which], recv_sem=sems.at[1, p, which],
            device_id=device, device_id_type=MESH,
        )
        copy.start()
        return copy

    def half_of(p, c):
        return pl.ds(pl.multiple_of((2 * p + c) * chips * rows, 8), chips * rows)

    def row_of(p):
        return pl.ds(pl.multiple_of(((2 * p + core) * chips + chip) * rows, 8), rows)

    def lane_of(i):
        return pl.ds(pl.multiple_of(i * width, 128), width)

    first_t, first_s = 1, len(sides) + 1
    again = len(sides) + len(stack) + 1
    flying = [[] for _ in range(PIECES)]
    sent = []

    def stage(p, number):
        for copy in flying[p]:
            copy.wait_recv()
        sent.extend(flying[p])
        flying[p] = []
        if number == 0:
            flying[p] = [send(grads.at[half_of(p, 1 - core)], land_c.at[p], p, 0, twin)]
        if number == 1:
            half[p] = grads[half_of(p, core)] + land_c[p]
            flying[p] = [
                send(half.at[p, pl.ds(pl.multiple_of(t * rows, 8), rows)], land_t.at[p, i], p, first_t + i, device)
                for i, (t, device) in enumerate(zip(peer_t, sides))
            ]
        if number == 2:
            total = half[p, pl.ds(pl.multiple_of(chip * rows, 8), rows)]
            for i in range(len(sides)):
                total += land_t[p, i]
            part[p] = total
            flying[p] = [
                send(part.at[p, :, lane_of(t)], land_s.at[p, i], p, first_s + i, device)
                for i, (t, device) in enumerate(zip(peer_s, stack))
            ]
        if number == 3:
            mine = part[p, :, lane_of(level)]
            for i in range(len(stack)):
                mine += land_s[p, i]
            out[row_of(p), lane_of(level)] = mine
            spot = out.at[row_of(p), lane_of(level)]
            flying[p] = [send(spot, spot, p, again + first_s + i, device) for i, device in enumerate(stack)]
        if number == 4:
            spot = out.at[row_of(p)]
            flying[p] = [send(spot, spot, p, again + first_t + i, device) for i, device in enumerate(sides)]
        if number == 5:
            spot = out.at[half_of(p, core)]
            flying[p] = [send(spot, spot, p, again, twin)]

    for number in (0, 1):
        for p in range(PIECES):
            stage(p, number)
    for tick in range(2, 5 + PIECES + 2):
        for p in range(PIECES):
            number = tick - p
            if 2 <= number <= 6:
                stage(p, number)
    for copy in sent:
        copy.wait_send()


def vmem(count):
    return [pl.BlockSpec(memory_space=pltpu.VMEM)] * count


SMEM_SPEC = pl.BlockSpec(memory_space=pltpu.SMEM)
ANY_SPEC = pl.BlockSpec(memory_space=pl.ANY)
LIMIT = 60 * 1024 * 1024


def shape(dims, dtype=F32):
    return jax.ShapeDtypeStruct(dims, dtype)


def shards(blocks, slabs, populations, w_in, w_mid, w_out, cotangent, face_source, face_level, face_quadrant):
    cells = populations.shape[-1]
    hid = w_in.shape[0]
    pops, cot = (v.reshape(Q * cells // LANES, LANES) for v in (populations, cotangent))
    table = jnp.asarray(row_table())
    w_mid = w_mid[0]
    step = 8 * blocks * PIECES
    total_rows = -(-(hid + 2 * R) // step) * step
    parts = cells // CHUNK
    volume = pltpu.VMEM((R, cells), F32)
    tmp = pltpu.VMEM((R, A), F32)
    sheet_rows = 24
    params = pltpu.CompilerParams(vmem_limit_bytes=LIMIT)

    def exchange(sheets, which):
        count = 2 * REACH + 3
        return pl.pallas_call(
            functools.partial(exchange_kernel, blocks, slabs),
            out_shape=shape((count, sheet_rows, A)),
            in_specs=vmem(1),
            out_specs=vmem(1)[0],
            scratch_shapes=[pltpu.SemaphoreType.DMA((count,)), pltpu.SemaphoreType.DMA((count,))],
            compiler_params=pltpu.CompilerParams(collective_id=which, has_side_effects=True),
            name=f"exchange{which}",
        )(sheets)

    post1, hidden, sheets, pick, w_in, w_in_t, w_out, w_out_t, w_mid_t = pl.pallas_call(
        first_kernel,
        out_shape=(
            shape((R, cells)), shape((2, hid, cells), BF16), shape((3, sheet_rows, A)), shape((6, A, A), BF16),
            shape((hid, R), BF16), shape((R, hid), BF16), shape((R, hid), BF16), shape((hid, R), BF16),
            shape((hid, hid), BF16),
        ),
        in_specs=[SMEM_SPEC] * 2 + vmem(6),
        out_specs=(vmem(1)[0], ANY_SPEC, *vmem(7)),
        scratch_shapes=[
            volume, volume, pltpu.VMEM((2, hid, cells), BF16), pltpu.VMEM((R, hid), F32),
            pltpu.SemaphoreType.DMA((2, parts)),
        ],
        compiler_params=params,
        name="first",
    )(face_level, face_quadrant, table, pops, cot, w_in.T, w_mid, w_out)
    backs = (w_in_t, w_mid_t, w_out_t)
    recv = exchange(sheets, 0)
    post2, bar, sheets, grads = pl.pallas_call(
        functools.partial(middle_kernel, blocks),
        out_shape=(shape((R, cells)), shape((R, cells)), shape((3, sheet_rows, A)), shape((total_rows, hid))),
        in_specs=[SMEM_SPEC] + vmem(11),
        out_specs=tuple(vmem(4)),
        scratch_shapes=[volume] * 4 + [tmp],
        compiler_params=params,
        name="middle",
    )(face_source.T, table, pick, recv, post1, cot, w_in, w_mid, w_out, *backs)
    recv = exchange(sheets, 1)
    final, grad_pops, grads = pl.pallas_call(
        functools.partial(last_kernel, blocks),
        out_shape=(shape(pops.shape), shape(pops.shape), shape((total_rows, hid))),
        in_specs=[SMEM_SPEC] + vmem(6) + [ANY_SPEC] + vmem(4),
        out_specs=tuple(vmem(3)),
        scratch_shapes=[volume] * 3 + [tmp, pltpu.VMEM((2, hid, cells), BF16), pltpu.SemaphoreType.DMA((2, parts))],
        compiler_params=params,
        name="last",
    )(face_source.T, table, pick, recv, post2, bar, pops, hidden, grads, *backs)
    chips = blocks // 2
    rows, width = total_rows // (blocks * PIECES), hid // slabs
    total = pl.pallas_call(
        functools.partial(sum_kernel, chips, slabs),
        out_shape=shape((total_rows, hid)),
        in_specs=vmem(1),
        out_specs=vmem(1)[0],
        scratch_shapes=[
            pltpu.VMEM((PIECES, chips * rows, hid), F32),
            pltpu.VMEM((PIECES, chips * rows, hid), F32),
            pltpu.VMEM((PIECES, chips - 1, rows, hid), F32),
            pltpu.VMEM((PIECES, rows, hid), F32),
            pltpu.VMEM((PIECES, slabs - 1, rows, width), F32),
            pltpu.SemaphoreType.DMA((2, PIECES, 2 * (chips + slabs - 1))),
        ],
        compiler_params=pltpu.CompilerParams(collective_id=2, has_side_effects=True),
        name="sum_all",
    )(grads)
    total = total * float(blocks * slabs * cells) ** (-0.5)
    return (
        final.reshape(populations.shape),
        grad_pops.reshape(populations.shape),
        total[hid : hid + Q].T,
        total[:hid][None],
        total[hid + R : hid + R + Q],
    )


def solution(mesh):
    spread = P(None, "slab", "blocks", None)
    in_specs = (spread, P(), P(), P(), spread, P(), P("slab", "blocks", None), P("slab", "blocks", None))
    out_specs = (spread, spread, P(), P(), P())
    body = functools.partial(shards, mesh.shape["blocks"], mesh.shape["slab"])
    return jax.shard_map(body, mesh=mesh, in_specs=in_specs, out_specs=out_specs, check_vma=False)
```

profile of v0, /device:TPU:0, one launch (start us, length us, event | category | flops | bytes accessed | tf_op | source)
XLA Modules:
  0.0 100.0 jit_solution(16810472117545681957)
XLA Ops:
  0.6 9.3 %first.1 = (f32[24,4096]{1,0:T(8,128)}, bf16[2,512,4096]{2,1,0:T(8,128)(2,1)}, f32[3,24,256]{2,1,0:T(8,128)}, bf16[6,256,256]{2,1,0:T(8,128)(2,1)}, bf16[512,24]...) custom-call(s32[1,1,6]{2,1,0:T(1,128)} %level.1, ...), custom_call_target="tpu_custom_call" | custom-call | tf_op jit(solution)/shard_map/first/pallas_call | solution.py:570
  10.0 11.4 %exchange0.1.recv = f32[9,24,256]{2,1,0:T(8,128)} custom-call(f32[3,24,256]{2,1,0:T(8,128)} %get-tuple-element.22.sheets), custom_call_target="tpu_custom_call" | custom-call | tf_op jit(solution)/shard_map/exchange0/pallas_call | solution.py:560
  21.3 20.0 %middle.1 = (f32[24,4096]{1,0:T(8,128)}, f32[24,4096]{1,0:T(8,128)}, f32[3,24,256]{2,1,0:T(8,128)}, f32[576,512]{1,0:T(8,128)}) custom-call(s32[4,8]{1,0:T(4,128)} %bitcast.18, s32[4,24,256]{2,1,0:T(8,128)} %constant.4.clone.table, bf16[6,256,256]{2,1,0:T(8,128)(2,1)} %get-tuple-element.21.pick, f32[9,24,256]{2,1,0:T(8,128)} %exchange0.1.recv, ...), custom_call_target="tpu_custom_call" | custom-call | tf_op jit(solution)/shard_map/middle/pallas_call | solution.py:588
  41.4 7.7 %exchange1.1.recv = f32[9,24,256]{2,1,0:T(8,128)} custom-call(f32[3,24,256]{2,1,0:T(8,128)} %get-tuple-element.29.sheets), custom_call_target="tpu_custom_call" | custom-call | tf_op jit(solution)/shard_map/exchange1/pallas_call | solution.py:560
  49.1 16.7 %last.1 = (f32[608,128]{1,0:T(8,128)}, f32[608,128]{1,0:T(8,128)}, f32[576,512]{1,0:T(8,128)}) custom-call(s32[4,8]{1,0:T(4,128)} %bitcast.19, s32[4,24,256]{2,1,0:T(8,128)} %constant.4.clone.table, bf16[6,256,256]{2,1,0:T(8,128)(2,1)} %get-tuple-element.21.pick, f32[9,24,256]{2,1,0:T(8,128)} %exchange1.1.recv, f32[24,4096]{1,0:T(8,128)} %get-tuple-element.30.post2, ...), custom_call_target="tpu_custom_call" | custom-call | tf_op jit(solution)/shard_map/last/pallas_call | solution.py:598
  65.8 31.1 %sum_all.1 = f32[576,512]{1,0:T(8,128)} custom-call(f32[576,512]{1,0:T(8,128)} %get-tuple-element.36.grads), custom_call_target="tpu_custom_call" | custom-call | tf_op jit(solution)/shard_map/sum_all/pallas_call | solution.py:609
  96.9 1.4 %broadcast_multiply_fusion = f32[576,512]{1,0:T(8,128)S(1)} fusion(f32[576,512]{1,0:T(8,128)} %sum_all.1), kind=kLoop, calls=%fused_computation.1 | loop fusion | flops 294912 | bytes 2359296 | tf_op jit(solution)/shard_map/mul | solution.py:625
  98.3 0.6 fusion
  98.9 1.0 %slice_bitcast_fusion = f32[1,512,512]{2,1,0:T(8,128)} fusion(f32[576,512]{1,0:T(8,128)S(1)} %broadcast_multiply_fusion), kind=kLoop, calls=%fused_computation | loop fusion | bytes 2097152 | tf_op jit(solution)/shard_map/broadcast_in_dim | solution.py:630
where the time goes:
time: 100 us
  Pallas kernels  96.2 us (96%)
  local copies, waits for them, and re-layouts  1.68 us (2%)
  other arithmetic  1.4 us (1%)
    pallas_call x1, Pallas kernels, shards(): pl.pallas_call(functools.partial(sum_kernel, chips, slabs), out_shape=sha...  31.1 us
    pallas_call x1, Pallas kernels, shards(): pl.pallas_call(functools.partial(middle_kernel, blocks), out_shape=(shape...  20 us
    pallas_call x2, Pallas kernels, exchange(): pl.pallas_call(functools.partial(exchange_kernel, blocks, slabs), out_sha...  19.1 us
    pallas_call x1, Pallas kernels, shards(): pl.pallas_call(functools.partial(last_kernel, blocks), out_shape=(shape(p...  16.7 us
    pallas_call x1, Pallas kernels, shards(): pl.pallas_call(first_kernel, out_shape=(shape((R, cells)), shape((2, hid,...  9.32 us

commit v1 on v0

v1 whole, which is shorter than its diff:
```python
import functools

import jax
import jax.numpy as jnp
from jax import lax
from jax.experimental import pallas as pl
from jax.experimental.pallas import tpu as pltpu
from jax.sharding import PartitionSpec as P

REACH = 3
R = 24
S = 16
A = S * S
LANES = 128
HALVES = A // LANES
CHUNK = 1024
LINES = CHUNK // LANES
BLOCK = S + 2
PITCH = HALVES * BLOCK
ROWS = R * PITCH
MESH = pl.DeviceIdType.MESH
F32, BF16 = jnp.float32, jnp.bfloat16

VELOCITIES = [
    (0, 0, 0),
    (1, 0, 0),
    (-1, 0, 0),
    (0, 1, 0),
    (0, -1, 0),
    (0, 0, 1),
    (0, 0, -1),
    (1, 1, 0),
    (-1, -1, 0),
    (1, -1, 0),
    (-1, 1, 0),
    (1, 0, 1),
    (-1, 0, -1),
    (1, 0, -1),
    (-1, 0, 1),
    (0, 1, 1),
    (0, -1, -1),
    (0, 1, -1),
    (0, -1, 1),
]
Q = len(VELOCITIES)
OPPOSITE = [VELOCITIES.index((-a, -b, -c)) for a, b, c in VELOCITIES]
FACED = 5
SHEET = 2 * HALVES * FACED
SHEET_ROWS = 24


def members(axis, side):
    return [q for q, v in enumerate(VELOCITIES) if v[axis] == (1, -1)[side]]


def place(q, axis):
    side = 0 if VELOCITIES[q][axis] == 1 else 1
    return side, members(axis, side).index(q)


def base(q, half):
    return q * PITCH + half * BLOCK + 1


def load(ref, q, half, off=0):
    return ref[pl.ds(base(q, half) + off, S), :]


def save(ref, q, half, value):
    ref[pl.ds(base(q, half), S), :] = value


def get_lines(ref, i):
    first = i * (LINES // HALVES)
    return jnp.concatenate(
        [ref[pl.ds(j % HALVES * BLOCK + 1 + j // HALVES + first, R, stride=PITCH), :] for j in range(LINES)], axis=1
    )


def put_lines(ref, i, value):
    first = i * (LINES // HALVES)
    for j in range(LINES):
        at = pl.ds(j % HALVES * BLOCK + 1 + j // HALVES + first, R, stride=PITCH)
        ref[at, :] = value[:, j * LANES : (j + 1) * LANES]


def from_cells(dst, src):
    for q in range(Q):
        for half in range(HALVES):
            save(dst, q, half, src[pl.ds(q * S * HALVES + half, S, stride=HALVES), :])


def to_cells(dst, q, half, value):
    dst[pl.ds(q * S * HALVES + half, S, stride=HALVES), :] = value


class Grid:
    def __init__(self):
        self.x = lax.broadcasted_iota(jnp.int32, (S, LANES), 0)
        self.lane = lax.broadcasted_iota(jnp.int32, (S, LANES), 1)
        self.y = self.lane // S
        self.z = self.lane % S
        self.lane1 = lax.broadcasted_iota(jnp.int32, (1, LANES), 1)
        self.y1, self.z1 = self.lane1 // S, self.lane1 % S


def roll(x, shift):
    shift %= LANES
    return x if shift == 0 else pltpu.roll(x, shift, 1)


def fan(x, shift, stride):
    return pltpu.roll(x, shift % LANES, 1, stride=stride, stride_axis=0)


def carry(g, pair, step, lane):
    if step == 1:
        return [pair[0], jnp.where(lane < LANES - S, pair[1], pair[0])]
    if step == -1:
        return [jnp.where(lane >= S, pair[0], pair[1]), pair[1]]
    return pair


def wide(row):
    return jnp.broadcast_to(row, (8, LANES))


def spread_y(row_of, side):
    shift = 0 if side == 0 else -(LANES - S)
    return jnp.concatenate([fan(wide(row_of(half)), shift, S) for half in range(HALVES)], axis=0)


def spread_z(g, row_of, z, dy):
    pair = carry(g, [row_of(half) for half in range(HALVES)], dy, g.lane1)
    return [
        jnp.concatenate([fan(wide(row), z - (S - 1) + S * dy + 8 * part, 1) for part in range(2)], axis=0) for row in pair
    ]


def total_rows(x):
    return jnp.sum(x, axis=0, keepdims=True)


def sheet_row(side, half, r):
    return (side * HALVES + half) * FACED + r


def put_row(ref, side, half, r, value):
    at = sheet_row(side, half, r)
    ref[at : at + 1, :] = value


def fold_y(x, high):
    shift = S if high else 0
    return [total_rows(fan(x[8 * part : 8 * part + 8], shift, S)) for part in range(2)]


def fold_z(x, z):
    return total_rows(sum(fan(x[8 * part : 8 * part + 8], 8 * part - z, 1) for part in range(2)))


def gather_sheets(g, post, sheets):
    for q, v in enumerate(VELOCITIES):
        if v[0]:
            side, r = place(q, 0)
            for half in range(HALVES):
                at = base(q, half) + (S - 1 if v[0] == 1 else 0)
                put_row(sheets.at[0], side, half, r, post[at : at + 1, :])
        if v[1]:
            side, r = place(q, 1)
            high = v[1] == 1
            x = jnp.where(g.y == (7 if high else 0), load(post, q, 1 if high else 0), 0.0)
            for part, row in enumerate(fold_y(x, high)):
                put_row(sheets.at[1], side, part, r, row)
        if v[2]:
            side, r = place(q, 2)
            z = S - 1 if v[2] == 1 else 0
            for half in range(HALVES):
                row = fold_z(jnp.where(g.z == z, load(post, q, half), 0.0), z)
                put_row(sheets.at[2], side, half, r, row)


def inside_z(z, dz):
    return z != (0 if dz == 1 else S - 1)


def gather_bars(g, bar, tmp):
    last = LANES // S - 1
    for q, (dx, dy, dz) in enumerate(VELOCITIES):
        if dx:
            side, r = place(q, 0)
            rows = []
            for half in range(HALVES):
                at = base(q, half) + (0 if dx == 1 else S - 1)
                row = bar[at : at + 1, :]
                rows.append(jnp.where(inside_z(g.z1, dz), row, 0.0) if dz else row)
            rows = [roll(row, -S * dy - dz) for row in carry(g, rows, -dy, g.lane1)]
            if dy:
                half, y = (1, last) if dy == 1 else (0, 0)
                rows[half] = jnp.where(g.y1 == y, 0.0, rows[half])
            for half in range(HALVES):
                put_row(tmp.at[0], side, half, r, rows[half])
        if dy:
            side, r = place(q, 1)
            keep = g.y == (0 if dy == 1 else last)
            if dz:
                keep &= inside_z(g.z, dz)
            if dx:
                keep &= g.x != (S - 1 if dx == 1 else 0)
            x = jnp.where(keep, load(bar, q, 0 if dy == 1 else 1, dx), 0.0)
            for part, row in enumerate(fold_y(x, dy == -1)):
                put_row(tmp.at[1], side, part, r, roll(row, -dz))
        if dz:
            side, r = place(q, 2)
            z = 0 if dz == 1 else S - 1
            rows = []
            for half in range(HALVES):
                keep = g.z == z
                if dx:
                    keep &= g.x != (S - 1 if dx == 1 else 0)
                if dy and half == (0 if dy == 1 else 1):
                    keep &= g.y != (0 if dy == 1 else last)
                rows.append(fold_z(jnp.where(keep, load(bar, q, half, dx), 0.0), z))
            rows = [roll(row, -S * dy) for row in carry(g, rows, -dy, g.lane1)]
            if dy:
                half, y = (1, last) if dy == 1 else (0, 0)
                rows[half] = jnp.where(g.y1 == y, 0.0, rows[half])
            for half in range(HALVES):
                put_row(tmp.at[2], side, half, r, rows[half])


def refined(halves, pick, transposed):
    sheet = jnp.concatenate(halves, axis=1)
    hi = sheet.astype(BF16).astype(F32)
    rest = sheet - hi
    mid = rest.astype(BF16).astype(F32)
    parts = jnp.concatenate([hi, mid, rest - mid], axis=0).astype(BF16)
    dims = (((1,), (1 if transposed else 0,)), ((), ()))
    r = lax.dot_general(parts, pick, dims, preferred_element_type=F32)
    return r[:8] + r[8:16] + r[16:]


def sheet_halves(ref, side):
    return [ref[pl.ds(sheet_row(side, half, 0), 8), :] for half in range(HALVES)]


def send_bars(g, bar, tmp, sheets, picks):
    gather_bars(g, bar, tmp)
    for axis in range(3):
        for side in range(2):
            out = refined(sheet_halves(tmp.at[axis], side), picks[pick_at(axis, side, True)], True)
            for half in range(HALVES):
                sheets[axis, pl.ds(sheet_row(side, half, 0), FACED), :] = out[:FACED, half * LANES : (half + 1) * LANES]


def pick_at(axis, side, back):
    if axis == 0:
        return side
    return 2 + 8 // 2 * back + 2 * (axis - 1) + side


def build_picks(level, quadrant, picks, back, axes):
    lane = lax.broadcasted_iota(jnp.int32, (1, A), 1)
    source = lax.broadcasted_iota(jnp.int32, (A, A), 0)
    half = S // 2

    def turned(axis, i):
        if axis == 0:
            return i
        if axis == 1:
            return i // LANES * LANES + (7 - i // S % 8) * S + i % S
        return i // S * S + (S - 1 - i % S)

    for axis in axes:
        for side in range(2):
            face = 2 * axis + 1 - side
            quad = quadrant[0, 0, face]
            first, second = quad // 2, quad % 2
            if axis == 2:
                first, second = second, first

            def wanted(i):
                fine = (first * half + i // S // 2) * S + second * half + i % S // 2
                return jnp.where(level[0, 0, face] == 1, fine, i)

            want = turned(axis, wanted(lane)) if back else wanted(turned(axis, lane))
            picks[pick_at(axis, side, back)] = jnp.where(source == want, 1.0, 0.0).astype(BF16)


def slot_of(source, blocks, face):
    me = lax.axis_index("blocks")
    distance = lax.rem(source[face, me] - me + blocks, blocks)
    distance = jnp.where(distance > blocks // 2, distance - blocks, distance)
    slot = jnp.where(distance < 0, distance + REACH, distance + REACH - 1)
    return jnp.clip(slot, 0, 2 * REACH - 1)


def ghost_row(axis, side, half, r):
    return (((axis - 1) * 2 + side) * HALVES + half) * 8 + r


def settle(recv, slots, picks, post, ghosts):
    for side in range(2):
        slot = slots[1 - side]
        halves = [recv[slot, pl.ds(sheet_row(side, half, 0), 8), :] for half in range(HALVES)]
        out = refined(halves, picks[pick_at(0, side, False)], False)
        for r, q in enumerate(members(0, side)):
            for half in range(HALVES):
                at = base(q, half) + (-1 if side == 0 else S)
                post[at : at + 1, :] = out[r : r + 1, half * LANES : (half + 1) * LANES]
    for axis in (1, 2):
        for side in range(2):
            slot = 2 * REACH if axis == 1 else 2 * REACH + (2 if side == 0 else 1)
            out = refined(sheet_halves(recv.at[slot], side), picks[pick_at(axis, side, False)], False)
            for half in range(HALVES):
                at = ghost_row(axis, side, half, 0)
                ghosts[at : at + 8, :] = out[:, half * LANES : (half + 1) * LANES]


def stream(g, post, ghosts, shifted, store):
    last = LANES // S - 1
    used = [0]

    def moved(value, dx):
        if not dx:
            return value
        at = used[0] * BLOCK + 1
        used[0] += 1
        shifted[pl.ds(at, S), :] = value
        return shifted[pl.ds(at - dx, S), :]

    for q, (dx, dy, dz) in enumerate(VELOCITIES):
        t = [load(post, q, half, -dx) for half in range(HALVES)]
        if dy:
            side, r = place(q, 1)

            def row_y(half):
                at = ghost_row(1, side, half, r)
                return ghosts[at : at + 1, :]

            halo = moved(spread_y(row_y, side), dx)
            if dy == 1:
                inner = g.lane < LANES - S
                t = [jnp.where(inner, t[0], halo), jnp.where(inner, t[1], t[0])]
            else:
                inner = g.lane >= S
                t = [jnp.where(inner, t[0], t[1]), jnp.where(inner, t[1], halo)]
        t = [roll(x, S * dy + dz) for x in t]
        if dz:
            side, r = place(q, 2)
            z = 0 if dz == 1 else S - 1

            def row_z(half):
                at = ghost_row(2, side, half, r)
                return ghosts[at : at + 1, :]

            halo = [moved(x, dx) for x in spread_z(g, row_z, z, dy)]
            t = [jnp.where(g.z == z, halo[half], t[half]) for half in range(HALVES)]
        for half in range(HALVES):
            two = crossed(g, half, dx, dy, dz)
            if two is not None:
                t[half] = jnp.where(two, load(post, OPPOSITE[q], half), t[half])
            store(q, half, t[half])


def crossed(g, half, dx, dy, dz):
    if (dx != 0) + (dy != 0) + (dz != 0) < 2:
        return None
    if dy and half != (0 if dy == 1 else 1):
        return None
    on = None
    for d, c, top in ((dx, g.x, S - 1), (dy, g.y, LANES // S - 1), (dz, g.z, S - 1)):
        if d:
            hit = c == (0 if d == 1 else top)
            on = hit if on is None else on & hit
    return on


def stream_back(g, bar, recv, slots, store):
    last = LANES // S - 1
    for q, (dx, dy, dz) in enumerate(VELOCITIES):
        t = [load(bar, q, half, dx) for half in range(HALVES)]
        t = [roll(x, -S * dy - dz) for x in carry(g, t, -dy, g.lane)]
        faces = []
        if dx:
            side, r = place(q, 0)
            slot = slots[side]
            rows = [recv[slot, pl.ds(sheet_row(side, half, r), 1), :] for half in range(HALVES)]
            rows = [jnp.broadcast_to(row, (S, LANES)) for row in rows]
            faces.append((rows, [g.x == (S - 1 if dx == 1 else 0)] * 2))
        if dy:
            side, r = place(q, 1)
            full = spread_y(lambda half: recv[2 * REACH, pl.ds(sheet_row(side, half, r), 1), :], side)
            mask = g.y == (last if dy == 1 else 0)
            faces.append(([full, full], [mask if half == (1 if dy == 1 else 0) else None for half in range(HALVES)]))
        if dz:
            side, r = place(q, 2)
            slot = 2 * REACH + (1 if side == 0 else 2)
            z = S - 1 if dz == 1 else 0
            full = spread_z(g, lambda half: recv[slot, pl.ds(sheet_row(side, half, r), 1), :], z, 0)
            faces.append((full, [g.z == z] * 2))
        for half in range(HALVES):
            here = [(value[half], mask[half]) for value, mask in faces if mask[half] is not None]
            out = t[half]
            if len(here) == 1:
                out = jnp.where(here[0][1], here[0][0], out)
            if len(here) == 2:
                (va, ma), (vb, mb) = here
                both = va + vb + load(bar, OPPOSITE[q], half)
                out = jnp.where(mb, jnp.where(ma, both, vb), jnp.where(ma, va, out))
            store(q, half, out)


def mm(a, b):
    return jnp.dot(a, b, preferred_element_type=F32)


def outer(a, b):
    return lax.dot_general(a, b, (((1,), (1,)), ((), ())), preferred_element_type=F32)


def slope(h):
    wide_h = h.astype(F32)
    return 1.0 - wide_h * wide_h


def span(i):
    return pl.ds(pl.multiple_of(i * CHUNK, CHUNK), CHUNK)


def padded_rows(src, tall, flat, flipped):
    tall[...] = jnp.zeros(tall.shape, F32)
    tall[:Q] = src[...].astype(F32)
    flat[...] = tall[...].astype(BF16)
    flipped[...] = tall[...].T.astype(BF16)


OFFSETS = [d for d in range(-REACH, REACH + 1) if d != 0]


class Exchange:
    def __init__(self, blocks, slabs):
        me, level = lax.axis_index("blocks"), lax.axis_index("slab")
        self.side = [lax.rem(me - d + blocks, blocks) for d in OFFSETS]
        self.other = me + 1 - 2 * lax.rem(me, 2)
        self.above, self.below = lax.rem(level + 1, slabs), lax.rem(level + slabs - 1, slabs)

    def greet(self):
        barrier = pltpu.get_barrier_semaphore()
        for target in self.side:
            pl.semaphore_signal(barrier, inc=1, device_id={"blocks": target}, device_id_type=MESH)
        for target in (self.above, self.below):
            pl.semaphore_signal(barrier, inc=1, device_id={"slab": target}, device_id_type=MESH)

    def meet(self):
        pl.semaphore_wait(pltpu.get_barrier_semaphore(), len(self.side) + 2)

    def send(self, sheets, recv, sems):
        plan = [(0, i, {"blocks": target}) for i, target in enumerate(self.side)]
        plan.append((1, 2 * REACH, {"blocks": self.other}))
        plan.append((2, 2 * REACH + 1, {"slab": self.below}))
        plan.append((2, 2 * REACH + 2, {"slab": self.above}))
        copies = []
        for which, slot, device in sorted(plan, key=lambda row: -row[0]):
            copy = pltpu.make_async_remote_copy(
                src_ref=sheets.at[which, pl.ds(0, SHEET)], dst_ref=recv.at[slot, pl.ds(0, SHEET)],
                send_sem=sems.at[0, slot], recv_sem=sems.at[1, slot],
                device_id=device, device_id_type=MESH,
            )
            copy.start()
            copies.append(copy)
        return copies


def arrive(copies):
    for copy in copies:
        copy.wait_recv()


def step_kernel(
    blocks, slabs, source, level, quadrant, pops, cot, w_in_rows, w_mid, w_out_rows,
    final, grad_pops, grads,
    fa, fb, ca, cb, x1, x2, e, h0a, h1a, h0b, h1b, a1, a0,
    sheets0, sheets1, sheets2, sheets3, recv0, recv1, recv2, recv3, tmp, ghosts, shifted, picks, w_in, w_in_t, w_out, w_out_t, w_mid_t, tall, sems,
):
    g = Grid()
    cells = x1.shape[1]
    hid = w_mid.shape[0]
    chunks = cells // CHUNK
    for ref in (recv0, recv1, recv2, recv3):
        ref[:, SHEET:, :] = jnp.zeros((ref.shape[0], SHEET_ROWS - SHEET, LANES), F32)
    link = Exchange(blocks, slabs)
    link.greet()
    slots = [slot_of(source, blocks, face) for face in (0, 1)]
    for ref in (fa, fb, cb):
        ref[Q * PITCH :, :] = jnp.zeros((ROWS - Q * PITCH, LANES), F32)
    tmp[...] = jnp.zeros(tmp.shape, F32)

    from_cells(ca, cot)
    build_picks(level, quadrant, picks, True, (0, 1, 2))
    send_bars(g, ca, tmp, sheets0, picks)
    link.meet()
    bars2 = link.send(sheets0, recv0, sems.at[0])

    padded_rows(w_in_rows, tall, w_in_t, w_in)
    padded_rows(w_out_rows, tall, w_out, w_out_t)
    from_cells(fa, pops)

    def forward(f, x, h0, h1):
        @pl.loop(0, chunks)
        def _(i):
            at = span(i)
            state = get_lines(f, i)
            inputs = state.astype(BF16)
            x[:, at] = inputs
            first = jnp.tanh(mm(w_in[...], inputs)).astype(BF16)
            h0[:, at] = first
            second = jnp.tanh(mm(w_mid[...], first)).astype(BF16)
            h1[:, at] = second
            put_lines(f, i, state + mm(w_out[...], second))

    def backward(p, h0, h1):
        @pl.loop(0, chunks)
        def _(i):
            at = span(i)
            bar = get_lines(p, i)
            err = bar.astype(BF16)
            e[:, at] = err
            second = (mm(w_out_t[...], err) * slope(h1[:, at])).astype(BF16)
            a1[:, at] = second
            first = (mm(w_mid_t[...], second) * slope(h0[:, at])).astype(BF16)
            a0[:, at] = first
            put_lines(p, i, bar + mm(w_in_t[...], first))

    def weights(x, h0, h1, old):
        for at, left, right in (
            (0, a1.at[: hid // 2], h0),
            (hid // 2, a1.at[hid // 2 :], h0),
            (hid, x, a0),
            (hid + R, e, h1),
        ):
            value = outer(left[...], right[...])
            spot_rows = pl.ds(at, value.shape[0])
            grads[spot_rows] = grads[spot_rows] + value if old else value

    forward(fa, x1, h0a, h1a)
    gather_sheets(g, fa, sheets1)
    posts1 = link.send(sheets1, recv1, sems.at[1])
    w_mid_t[...] = w_mid[...].astype(F32).T.astype(BF16)
    build_picks(level, quadrant, picks, False, (1, 2))
    arrive(bars2)
    stream_back(g, ca, recv0, slots, functools.partial(save, cb))
    arrive(posts1)
    settle(recv1, slots, picks, fa, ghosts)
    stream(g, fa, ghosts, shifted, functools.partial(save, fb))

    forward(fb, x2, h0b, h1b)
    gather_sheets(g, fb, sheets2)
    posts2 = link.send(sheets2, recv2, sems.at[2])
    backward(cb, h0b, h1b)
    send_bars(g, cb, tmp, sheets3, picks)
    bars1 = link.send(sheets3, recv3, sems.at[3])
    grads[...] = jnp.zeros(grads.shape, F32)
    weights(x2, h0b, h1b, False)
    arrive(posts2)
    settle(recv2, slots, picks, fb, ghosts)
    stream(g, fb, ghosts, shifted, functools.partial(to_cells, final))
    arrive(bars1)
    stream_back(g, cb, recv3, slots, functools.partial(save, fa))
    backward(fa, h0a, h1a)
    weights(x1, h0a, h1a, True)
    for q in range(Q):
        for half in range(HALVES):
            to_cells(grad_pops, q, half, load(fa, q, half))
    for copies in (bars2, posts1, posts2, bars1):
        for copy in copies:
            copy.wait_send()


PIECES = 3


def sum_kernel(chips, slabs, grads, out, land_c, half, land_t, part, land_s, sems):
    me, level = lax.axis_index("blocks"), lax.axis_index("slab")
    core, chip = lax.rem(me, 2), me // 2
    rows, width = part.shape[1], land_s.shape[-1]
    peer_t = [lax.rem(chip + d, chips) for d in range(1, chips)]
    peer_s = [lax.rem(level + d, slabs) for d in range(1, slabs)]
    twin = {"blocks": me + 1 - 2 * core}
    sides = [{"blocks": 2 * t + core} for t in peer_t]
    stack = [{"slab": t} for t in peer_s]
    barrier = pltpu.get_barrier_semaphore()
    for device in [twin] + sides + stack:
        pl.semaphore_signal(barrier, inc=1, device_id=device, device_id_type=MESH)
    pl.semaphore_wait(barrier, 1 + len(sides) + len(stack))

    def send(src, dst, p, which, device):
        copy = pltpu.make_async_remote_copy(
            src_ref=src, dst_ref=dst, send_sem=sems.at[0, p, which], recv_sem=sems.at[1, p, which],
            device_id=device, device_id_type=MESH,
        )
        copy.start()
        return copy

    def half_of(p, c):
        return pl.ds(pl.multiple_of((2 * p + c) * chips * rows, 8), chips * rows)

    def row_of(p):
        return pl.ds(pl.multiple_of(((2 * p + core) * chips + chip) * rows, 8), rows)

    def lane_of(i):
        return pl.ds(pl.multiple_of(i * width, 128), width)

    first_t, first_s = 1, len(sides) + 1
    again = len(sides) + len(stack) + 1
    flying = [[] for _ in range(PIECES)]
    sent = []

    def stage(p, number):
        for copy in flying[p]:
            copy.wait_recv()
        sent.extend(flying[p])
        flying[p] = []
        if number == 0:
            flying[p] = [send(grads.at[half_of(p, 1 - core)], land_c.at[p], p, 0, twin)]
        if number == 1:
            half[p] = grads[half_of(p, core)] + land_c[p]
            flying[p] = [
                send(half.at[p, pl.ds(pl.multiple_of(t * rows, 8), rows)], land_t.at[p, i], p, first_t + i, device)
                for i, (t, device) in enumerate(zip(peer_t, sides))
            ]
        if number == 2:
            total = half[p, pl.ds(pl.multiple_of(chip * rows, 8), rows)]
            for i in range(len(sides)):
                total += land_t[p, i]
            part[p] = total
            flying[p] = [
                send(part.at[p, :, lane_of(t)], land_s.at[p, i], p, first_s + i, device)
                for i, (t, device) in enumerate(zip(peer_s, stack))
            ]
        if number == 3:
            mine = part[p, :, lane_of(level)]
            for i in range(len(stack)):
                mine += land_s[p, i]
            out[row_of(p), lane_of(level)] = mine
            spot = out.at[row_of(p), lane_of(level)]
            flying[p] = [send(spot, spot, p, again + first_s + i, device) for i, device in enumerate(stack)]
        if number == 4:
            spot = out.at[row_of(p)]
            flying[p] = [send(spot, spot, p, again + first_t + i, device) for i, device in enumerate(sides)]
        if number == 5:
            spot = out.at[half_of(p, core)]
            flying[p] = [send(spot, spot, p, again, twin)]

    for number in (0, 1):
        for p in range(PIECES):
            stage(p, number)
    for tick in range(2, 5 + PIECES + 2):
        for p in range(PIECES):
            number = tick - p
            if 2 <= number <= 6:
                stage(p, number)
    for copy in sent:
        copy.wait_send()


def vmem(count):
    return [pl.BlockSpec(memory_space=pltpu.VMEM)] * count


SMEM_SPEC = pl.BlockSpec(memory_space=pltpu.SMEM)
LIMIT = 60 * 1024 * 1024


def shape(dims, dtype=F32):
    return jax.ShapeDtypeStruct(dims, dtype)


def shards(blocks, slabs, populations, w_in, w_mid, w_out, cotangent, face_source, face_level, face_quadrant):
    cells = populations.shape[-1]
    hid = w_in.shape[0]
    pops, cot = (v.reshape(Q * cells // LANES, LANES) for v in (populations, cotangent))
    w_mid = w_mid[0]
    step = 8 * blocks * PIECES
    total_rows = -(-(hid + 2 * R) // step) * step
    volume = pltpu.VMEM((ROWS, LANES), F32)
    thin = pltpu.VMEM((R, cells), BF16)
    deep = pltpu.VMEM((hid, cells), BF16)
    slots = 2 * REACH + 3
    final, grad_pops, grads = pl.pallas_call(
        functools.partial(step_kernel, blocks, slabs),
        out_shape=(shape(pops.shape), shape(pops.shape), shape((total_rows, hid))),
        in_specs=[SMEM_SPEC] * 3 + vmem(5),
        out_specs=tuple(vmem(3)),
        scratch_shapes=[volume] * 4 + [thin] * 3 + [deep] * 6 + [
            *[pltpu.VMEM((3, SHEET_ROWS, LANES), F32)] * 4,
            *[pltpu.VMEM((slots, SHEET_ROWS, LANES), F32)] * 4,
            pltpu.VMEM((3, SHEET_ROWS, LANES), F32),
            pltpu.VMEM((4 * HALVES * 8, LANES), F32),
            pltpu.VMEM((16 * BLOCK, LANES), F32),
            pltpu.VMEM((10, A, A), BF16),
            pltpu.VMEM((hid, R), BF16),
            pltpu.VMEM((R, hid), BF16),
            pltpu.VMEM((R, hid), BF16),
            pltpu.VMEM((hid, R), BF16),
            pltpu.VMEM((hid, hid), BF16),
            pltpu.VMEM((R, hid), F32),
            pltpu.SemaphoreType.DMA((4, 2, slots)),
        ],
        compiler_params=pltpu.CompilerParams(vmem_limit_bytes=LIMIT, collective_id=0, has_side_effects=True),
        name="step",
    )(face_source.T, face_level, face_quadrant, pops, cot, w_in.T, w_mid, w_out)
    chips = blocks // 2
    rows, width = total_rows // (blocks * PIECES), hid // slabs
    total = pl.pallas_call(
        functools.partial(sum_kernel, chips, slabs),
        out_shape=shape((total_rows, hid)),
        in_specs=vmem(1),
        out_specs=vmem(1)[0],
        scratch_shapes=[
            pltpu.VMEM((PIECES, chips * rows, hid), F32),
            pltpu.VMEM((PIECES, chips * rows, hid), F32),
            pltpu.VMEM((PIECES, chips - 1, rows, hid), F32),
            pltpu.VMEM((PIECES, rows, hid), F32),
            pltpu.VMEM((PIECES, slabs - 1, rows, width), F32),
            pltpu.SemaphoreType.DMA((2, PIECES, 2 * (chips + slabs - 1))),
        ],
        compiler_params=pltpu.CompilerParams(collective_id=2, has_side_effects=True),
        name="sum_all",
    )(grads)
    total = total * float(blocks * slabs * cells) ** (-0.5)
    return (
        final.reshape(populations.shape),
        grad_pops.reshape(populations.shape),
        total[hid : hid + Q].T,
        total[:hid][None],
        total[hid + R : hid + R + Q],
    )


def solution(mesh):
    spread = P(None, "slab", "blocks", None)
    in_specs = (spread, P(), P(), P(), spread, P(), P("slab", "blocks", None), P("slab", "blocks", None))
    out_specs = (spread, spread, P(), P(), P())
    body = functools.partial(shards, mesh.shape["blocks"], mesh.shape["slab"])
    return jax.shard_map(body, mesh=mesh, in_specs=in_specs, out_specs=out_specs, check_vma=False)
```

time: 100 us -> 78.7 us (0.79)
  Pallas kernels: 96.2 us -> 73.3 us
  local copies, waits for them, and re-layouts: 1.68 us -> 3.13 us
    pallas_call x5 -> x1, Pallas kernels: 65.1 us -> 42.5 us  [shards(): pl.pallas_call(functools.partial(step_kernel, blocks, slabs), out_shape=(...]
    unnamed x0 -> x6, local copies, waits for them, and re-layouts: none -> 1.45 us
where the time goes in v1:
time: 78.7 us; the launch traced here: 78.5 us
  Pallas kernels  73.3 us (93%)
  local copies, waits for them, and re-layouts  3.13 us (4%)
  other arithmetic  1.4 us (2%)
    pallas_call x1, Pallas kernels, shards(): pl.pallas_call(functools.partial(step_kernel, blocks, slabs), out_shape=(...  42.5 us
    pallas_call x1, Pallas kernels, shards(): pl.pallas_call(functools.partial(sum_kernel, chips, slabs), out_shape=sha...  30.8 us

profile of v1, /device:TPU:0, one launch (start us, length us, event | category | flops | bytes accessed | tf_op | source)
XLA Modules:
  0.0 78.5 jit_solution(13155441251143172058)
XLA Ops:
  0.6 42.5 %step.1 = (f32[608,128]{1,0:T(8,128)}, f32[608,128]{1,0:T(8,128)}, f32[576,512]{1,0:T(8,128)}) custom-call(s32[4,8]{1,0:T(4,128)} %bitcast.17, s32[1,1,6]{2,1,0:T(1,128)} %level.1, s32[1,1,6]{2,1,0:T(1,128)} %quadrant.1, f32[608,128]{1,0:T(8,128)} %bitcast.12, f32[608,128]{1,0:T(8,128)} %bitcast.13, bf16[19,512]{1,0:T(8,128)(2,1)} %bitcast.16, ...), custom_call_target="tpu_custom_call" | custom-call | tf_op jit(solution)/shard_map/step/pallas_call | solution.py:690
  43.1 30.8 %sum_all.1 = f32[576,512]{1,0:T(8,128)} custom-call(f32[576,512]{1,0:T(8,128)} %get-tuple-element.10.grads), custom_call_target="tpu_custom_call" | custom-call | tf_op jit(solution)/shard_map/sum_all/pallas_call | solution.py:715
  73.9 1.4 %broadcast_multiply_fusion = f32[576,512]{1,0:T(8,128)S(1)} fusion(f32[576,512]{1,0:T(8,128)} %sum_all.1), kind=kLoop, calls=%fused_computation.1 | loop fusion | flops 294912 | bytes 2359296 | tf_op jit(solution)/shard_map/mul | solution.py:731
  75.3 0.0 copy-start.1
  75.3 0.6 fusion
  76.0 0.0 copy-start
  76.0 1.0 %slice_bitcast_fusion = f32[1,512,512]{2,1,0:T(8,128)} fusion(f32[576,512]{1,0:T(8,128)S(1)} %broadcast_multiply_fusion), kind=kLoop, calls=%fused_computation | loop fusion | bytes 2097152 | tf_op jit(solution)/shard_map/broadcast_in_dim | solution.py:736
  77.0 0.0 copy-done.1
  77.0 0.7 copy.19
  77.7 0.0 copy-done
  77.7 0.7 copy.20
Async XLA Ops:
  75.3 1.7 %copy-start.1 = (f32[608,128]{1,0:T(8,128)S(1)}, f32[608,128]{1,0:T(8,128)}, u32[]{:S(2)}) copy-start(f32[608,128]{1,0:T(8,128)} %get-tuple-element.8) | copy-start | bytes 933892
  76.0 1.8 %copy-start = (f32[608,128]{1,0:T(8,128)S(1)}, f32[608,128]{1,0:T(8,128)}, u32[]{:S(2)}) copy-start(f32[608,128]{1,0:T(8,128)} %get-tuple-element.9) | copy-start | bytes 933892

commit v2 on v1

--- a/solution.py
+++ b/solution.py
@@ -419,9 +419,9 @@
     return lax.dot_general(a, b, (((1,), (1,)), ((), ())), preferred_element_type=F32)
 
 
-def slope(h):
+def damp(u, h):
     wide_h = h.astype(F32)
-    return 1.0 - wide_h * wide_h
+    return (u * (1.0 - wide_h * wide_h)).astype(BF16)
 
 
 def span(i):
@@ -433,6 +433,114 @@
     tall[:Q] = src[...].astype(F32)
     flat[...] = tall[...].astype(BF16)
     flipped[...] = tall[...].T.astype(BF16)
+
+
+BIG = 4
+STAGES = 6
+
+
+class Total:
+    def __init__(self, blocks, slabs, hid, grads, out, land_c, half, land_a, tile, land_z, sems, scale):
+        self.me, self.level = lax.axis_index("blocks"), lax.axis_index("slab")
+        self.chips, self.pairs, self.scale = blocks // 2, slabs // 2, scale
+        self.count = self.chips * 2
+        self.core, self.chip = lax.rem(self.me, 2), self.me // 2
+        self.low, self.high = lax.rem(self.level, 2), self.level // 2
+        self.at = self.chip * 2 + self.low
+        self.grads, self.out, self.land_c, self.half = grads, out, land_c, half
+        self.land_a, self.tile, self.land_z, self.sems = land_a, tile, land_z, sems
+        self.hid = hid
+        self.rows = piece_rows(blocks, hid)
+        self.first = [sum(2 * n for n in self.rows[:p]) for p in range(len(self.rows))]
+        self.flying = [[] for _ in self.rows]
+        self.done = []
+
+    def go(self, p, src, dst, which, device):
+        copy = pltpu.make_async_remote_copy(
+            src_ref=src, dst_ref=dst, send_sem=self.sems.at[0, p, which], recv_sem=self.sems.at[1, p, which],
+            device_id=device, device_id_type=MESH,
+        )
+        copy.start()
+        self.flying[p].append(copy)
+        self.done.append(copy)
+
+    def settle(self, p):
+        for copy in self.flying[p]:
+            copy.wait_recv()
+        self.flying[p] = []
+
+    def rows_of(self, p, core):
+        n = self.rows[p]
+        return pl.ds(pl.multiple_of(self.first[p] + core * n, 8), n)
+
+    def size(self, p):
+        return part_size(self.rows[p], self.count, self.hid)
+
+    def part(self, p, t, start):
+        n, w = self.size(p)
+        across = self.hid // w
+        rows = pl.ds(pl.multiple_of(start + t // across * n, 8), n)
+        return rows, pl.ds(pl.multiple_of(lax.rem(t, across) * w, 128), w)
+
+    def twin(self):
+        return {"blocks": self.me + 1 - 2 * self.core}
+
+    def near(self):
+        for d in range(1, self.count):
+            t = lax.rem(self.at + d, self.count)
+            yield d - 1, t, {"blocks": t // 2 * 2 + self.core, "slab": self.high * 2 + lax.rem(t, 2)}
+
+    def far(self):
+        for d in range(1, self.pairs):
+            yield d - 1, {"slab": lax.rem(self.high + d, self.pairs) * 2 + self.low}
+
+    def friends(self):
+        return [device for _, _, device in self.near()] + [device for _, device in self.far()]
+
+    def stage(self, p, number):
+        n, w = self.size(p)
+        whole, small = pl.ds(0, self.rows[p]), (pl.ds(0, n), pl.ds(0, w))
+        tile = self.tile.at[p, *small]
+        again = self.count + self.pairs
+        start = self.first[p] + self.core * self.rows[p]
+        self.settle(p)
+        if number == 0:
+            self.go(p, self.grads.at[self.rows_of(p, 1 - self.core)], self.land_c.at[p, whole], 0, self.twin())
+        elif number == 1:
+            self.half[p, whole] = self.grads[self.rows_of(p, self.core)] + self.land_c[p, whole]
+            for i, t, device in self.near():
+                self.go(p, self.half.at[p, *self.part(p, t, 0)], self.land_a.at[p, i, *small], 1 + i, device)
+        elif number == 2:
+            total = self.half[p, *self.part(p, self.at, 0)]
+            for i in range(self.count - 1):
+                total += self.land_a[p, i, *small]
+            tile[...] = total
+            for i, device in self.far():
+                self.go(p, tile, self.land_z.at[p, i, *small], self.count + i, device)
+        elif number == 3:
+            total = tile[...]
+            for i in range(self.pairs - 1):
+                total += self.land_z[p, i, *small]
+            spot = self.out.at[*self.part(p, self.at, start)]
+            spot[...] = total * self.scale
+            for i, t, device in self.near():
+                self.go(p, spot, spot, again + i, device)
+        elif number == 4:
+            rows = self.out.at[self.rows_of(p, self.core)]
+            self.go(p, rows, rows, again + self.count, self.twin())
+
+    def close(self):
+        for copy in self.done:
+            copy.wait_send()
+
+
+def piece_rows(blocks, hid):
+    return [hid // BIG // 2] * BIG + [max(R + 8, blocks * 8 * LANES // hid)]
+
+
+def part_size(rows, count, hid):
+    n = max(rows // count, 8)
+    return n, rows // n * hid // count
 
 
 OFFSETS = [d for d in range(-REACH, REACH + 1) if d != 0]
@@ -444,6 +552,7 @@
         self.side = [lax.rem(me - d + blocks, blocks) for d in OFFSETS]
         self.other = me + 1 - 2 * lax.rem(me, 2)
         self.above, self.below = lax.rem(level + 1, slabs), lax.rem(level + slabs - 1, slabs)
+        self.friends = []
 
     def greet(self):
         barrier = pltpu.get_barrier_semaphore()
@@ -451,9 +560,11 @@
             pl.semaphore_signal(barrier, inc=1, device_id={"blocks": target}, device_id_type=MESH)
         for target in (self.above, self.below):
             pl.semaphore_signal(barrier, inc=1, device_id={"slab": target}, device_id_type=MESH)
+        for device in self.friends:
+            pl.semaphore_signal(barrier, inc=1, device_id=device, device_id_type=MESH)
 
     def meet(self):
-        pl.semaphore_wait(pltpu.get_barrier_semaphore(), len(self.side) + 2)
+        pl.semaphore_wait(pltpu.get_barrier_semaphore(), len(self.side) + 2 + len(self.friends))
 
     def send(self, sheets, recv, sems):
         plan = [(0, i, {"blocks": target}) for i, target in enumerate(self.side)]
@@ -478,11 +589,20 @@
 
 
 def step_kernel(
-    blocks, slabs, source, level, quadrant, pops, cot, w_in_rows, w_mid, w_out_rows,
-    final, grad_pops, grads,
-    fa, fb, ca, cb, x1, x2, e, h0a, h1a, h0b, h1b, a1, a0,
-    sheets0, sheets1, sheets2, sheets3, recv0, recv1, recv2, recv3, tmp, ghosts, shifted, picks, w_in, w_in_t, w_out, w_out_t, w_mid_t, tall, sems,
+    blocks, slabs, source, level, quadrant, pops_hbm, cot_hbm, w_in_hbm, w_mid_hbm, w_out_hbm,
+    final, grad_pops, out,
+    grads, land_c, half_c, land_a, tile, land_z, total_sems, fa, fb, ca, cb, x1, x2, e, h0a, h1a, h0b, h1b, a1, a0, u,
+    sheets0, sheets1, sheets2, sheets3, recv0, recv1, recv2, recv3, tmp, ghosts, shifted, picks, w_in, w_in_t, w_out, w_out_t, w_mid_t, tall,
+    pops, cot, w_in_rows, w_mid, w_out_rows, load_sems, sems,
 ):
+    loads = [
+        pltpu.make_async_copy(src, dst, load_sems.at[i])
+        for i, (src, dst) in enumerate(
+            ((cot_hbm, cot), (pops_hbm, pops), (w_in_hbm, w_in_rows), (w_out_hbm, w_out_rows), (w_mid_hbm, w_mid))
+        )
+    ]
+    for copy in loads:
+        copy.start()
     g = Grid()
     cells = x1.shape[1]
     hid = w_mid.shape[0]
@@ -490,18 +610,27 @@
     for ref in (recv0, recv1, recv2, recv3):
         ref[:, SHEET:, :] = jnp.zeros((ref.shape[0], SHEET_ROWS - SHEET, LANES), F32)
     link = Exchange(blocks, slabs)
+    total = Total(
+        blocks, slabs, hid, grads, out, land_c, half_c, land_a, tile, land_z, total_sems,
+        float(blocks * slabs * cells) ** (-0.5),
+    )
+    link.friends = total.friends()
+    second = hid + total.rows[BIG]
     link.greet()
     slots = [slot_of(source, blocks, face) for face in (0, 1)]
     for ref in (fa, fb, cb):
         ref[Q * PITCH :, :] = jnp.zeros((ROWS - Q * PITCH, LANES), F32)
     tmp[...] = jnp.zeros(tmp.shape, F32)
 
+    build_picks(level, quadrant, picks, True, (0, 1, 2))
+    loads[0].wait()
     from_cells(ca, cot)
-    build_picks(level, quadrant, picks, True, (0, 1, 2))
     send_bars(g, ca, tmp, sheets0, picks)
     link.meet()
     bars2 = link.send(sheets0, recv0, sems.at[0])
 
+    for copy in loads[1:]:
+        copy.wait()
     padded_rows(w_in_rows, tall, w_in_t, w_in)
     padded_rows(w_out_rows, tall, w_out, w_out_t)
     from_cells(fa, pops)
@@ -524,24 +653,39 @@
         def _(i):
             at = span(i)
             bar = get_lines(p, i)
-            err = bar.astype(BF16)
-            e[:, at] = err
-            second = (mm(w_out_t[...], err) * slope(h1[:, at])).astype(BF16)
+            second = damp(u[:, at], h1[:, at])
             a1[:, at] = second
-            first = (mm(w_mid_t[...], second) * slope(h0[:, at])).astype(BF16)
+            first = damp(mm(w_mid_t[...], second), h0[:, at])
             a0[:, at] = first
             put_lines(p, i, bar + mm(w_in_t[...], first))
 
-    def weights(x, h0, h1, old):
-        for at, left, right in (
-            (0, a1.at[: hid // 2], h0),
-            (hid // 2, a1.at[hid // 2 :], h0),
-            (hid, x, a0),
-            (hid + R, e, h1),
-        ):
-            value = outer(left[...], right[...])
-            spot_rows = pl.ds(at, value.shape[0])
-            grads[spot_rows] = grads[spot_rows] + value if old else value
+    def lift(p):
+        @pl.loop(0, chunks)
+        def _(i):
+            at = span(i)
+            err = get_lines(p, i).astype(BF16)
+            e[:, at] = err
+            u[:, at] = mm(w_out_t[...], err)
+
+    def top_down(h1, first, count):
+        rows = pl.ds(first, count)
+
+        @pl.loop(0, chunks)
+        def _(i):
+            at = span(i)
+            a1[rows, at] = damp(mm(w_out_t[rows], e[:, at]), h1[rows, at])
+
+    def bottom(p, h0, i):
+        at = pl.ds(i * CHUNK, CHUNK)
+        first = damp(mm(w_mid_t[...], a1[:, at]), h0[:, at])
+        a0[:, at] = first
+        put_lines(p, i, get_lines(p, i) + mm(w_in_t[...], first))
+
+    def weigh(first, left, right, old, columns=None):
+        value = outer(left[...], right[...])
+        spot_rows = pl.ds(first, value.shape[0])
+        at = (spot_rows, columns or slice(None))
+        grads[at] = grads[at] + value if old else value
 
     forward(fa, x1, h0a, h1a)
     gather_sheets(g, fa, sheets1)
@@ -550,6 +694,7 @@
     build_picks(level, quadrant, picks, False, (1, 2))
     arrive(bars2)
     stream_back(g, ca, recv0, slots, functools.partial(save, cb))
+    lift(cb)
     arrive(posts1)
     settle(recv1, slots, picks, fa, ghosts)
     stream(g, fa, ghosts, shifted, functools.partial(save, fb))
@@ -560,108 +705,69 @@
     backward(cb, h0b, h1b)
     send_bars(g, cb, tmp, sheets3, picks)
     bars1 = link.send(sheets3, recv3, sems.at[3])
-    grads[...] = jnp.zeros(grads.shape, F32)
-    weights(x2, h0b, h1b, False)
+    mid = hid // 2
+    grads[hid:] = jnp.zeros((grads.shape[0] - hid, hid), F32)
+    weigh(0, a1.at[:mid], h0b, False)
+    weigh(mid, a1.at[mid:], h0b, False)
+    weigh(hid, x2, a0, False)
+    weigh(second, e, h1b, False)
     arrive(posts2)
     settle(recv2, slots, picks, fb, ghosts)
     stream(g, fb, ghosts, shifted, functools.partial(to_cells, final))
     arrive(bars1)
     stream_back(g, cb, recv3, slots, functools.partial(save, fa))
-    backward(fa, h0a, h1a)
-    weights(x1, h0a, h1a, True)
+    for i in range(chunks):
+        e[:, i * CHUNK : (i + 1) * CHUNK] = get_lines(fa, i).astype(BF16)
+
+    def turns(*pairs):
+        pairs = pairs if isinstance(pairs[0], tuple) else (pairs,)
+        for p, number in pairs:
+            total.stage(p, number)
+
+    top_down(h1a, 0, mid)
+    weigh(0, a1.at[:mid], h0a, True)
+    turns((0, 0), (1, 0))
+    top_down(h1a, mid, mid)
+    weigh(mid, a1.at[mid:], h0a.at[:mid], True, slice(0, mid))
+    turns((0, 1), (1, 1))
+    weigh(mid, a1.at[mid:], h0a.at[mid:], True, slice(mid, hid))
+    turns((2, 0), (3, 0))
+    weigh(second, e, h1a, True)
+    turns((2, 1), (3, 1))
+    for i in range(chunks):
+        bottom(fa, h0a, i)
+    weigh(hid, x1, a0, True)
+    turns((BIG, 0))
     for q in range(Q):
         for half in range(HALVES):
             to_cells(grad_pops, q, half, load(fa, q, half))
+    turns((0, 2), (1, 2), (BIG, 1), (2, 2), (3, 2))
+    for number in range(3, STAGES):
+        turns((0, number), (1, number), (2, number), (3, number), (BIG, number - 1))
+    turns((BIG, STAGES - 1))
+    total.close()
     for copies in (bars2, posts1, posts2, bars1):
         for copy in copies:
             copy.wait_send()
 
 
-PIECES = 3
-
-
-def sum_kernel(chips, slabs, grads, out, land_c, half, land_t, part, land_s, sems):
-    me, level = lax.axis_index("blocks"), lax.axis_index("slab")
-    core, chip = lax.rem(me, 2), me // 2
-    rows, width = part.shape[1], land_s.shape[-1]
-    peer_t = [lax.rem(chip + d, chips) for d in range(1, chips)]
-    peer_s = [lax.rem(level + d, slabs) for d in range(1, slabs)]
-    twin = {"blocks": me + 1 - 2 * core}
-    sides = [{"blocks": 2 * t + core} for t in peer_t]
-    stack = [{"slab": t} for t in peer_s]
-    barrier = pltpu.get_barrier_semaphore()
-    for device in [twin] + sides + stack:
-        pl.semaphore_signal(barrier, inc=1, device_id=device, device_id_type=MESH)
-    pl.semaphore_wait(barrier, 1 + len(sides) + len(stack))
-
-    def send(src, dst, p, which, device):
-        copy = pltpu.make_async_remote_copy(
-            src_ref=src, dst_ref=dst, send_sem=sems.at[0, p, which], recv_sem=sems.at[1, p, which],
-            device_id=device, device_id_type=MESH,
-        )
+def leave_kernel(final, grad_pops, total, final_out, pops_out, mid_out, in_out, out_out, first_small, second_small, sems):
+    hid = mid_out.shape[0]
+    second = total.shape[0] - (total.shape[0] - hid) // 2
+    first_small[...] = total[hid : hid + Q, :]
+    second_small[...] = total[second : second + Q, :]
+    plan = [
+        (total.at[pl.ds(0, hid)], mid_out),
+        (final, final_out),
+        (grad_pops, pops_out),
+        (first_small, in_out),
+        (second_small, out_out),
+    ]
+    copies = [pltpu.make_async_copy(src, dst, sems.at[i]) for i, (src, dst) in enumerate(plan)]
+    for copy in copies:
         copy.start()
-        return copy
-
-    def half_of(p, c):
-        return pl.ds(pl.multiple_of((2 * p + c) * chips * rows, 8), chips * rows)
-
-    def row_of(p):
-        return pl.ds(pl.multiple_of(((2 * p + core) * chips + chip) * rows, 8), rows)
-
-    def lane_of(i):
-        return pl.ds(pl.multiple_of(i * width, 128), width)
-
-    first_t, first_s = 1, len(sides) + 1
-    again = len(sides) + len(stack) + 1
-    flying = [[] for _ in range(PIECES)]
-    sent = []
-
-    def stage(p, number):
-        for copy in flying[p]:
-            copy.wait_recv()
-        sent.extend(flying[p])
-        flying[p] = []
-        if number == 0:
-            flying[p] = [send(grads.at[half_of(p, 1 - core)], land_c.at[p], p, 0, twin)]
-        if number == 1:
-            half[p] = grads[half_of(p, core)] + land_c[p]
-            flying[p] = [
-                send(half.at[p, pl.ds(pl.multiple_of(t * rows, 8), rows)], land_t.at[p, i], p, first_t + i, device)
-                for i, (t, device) in enumerate(zip(peer_t, sides))
-            ]
-        if number == 2:
-            total = half[p, pl.ds(pl.multiple_of(chip * rows, 8), rows)]
-            for i in range(len(sides)):
-                total += land_t[p, i]
-            part[p] = total
-            flying[p] = [
-                send(part.at[p, :, lane_of(t)], land_s.at[p, i], p, first_s + i, device)
-                for i, (t, device) in enumerate(zip(peer_s, stack))
-            ]
-        if number == 3:
-            mine = part[p, :, lane_of(level)]
-            for i in range(len(stack)):
-                mine += land_s[p, i]
-            out[row_of(p), lane_of(level)] = mine
-            spot = out.at[row_of(p), lane_of(level)]
-            flying[p] = [send(spot, spot, p, again + first_s + i, device) for i, device in enumerate(stack)]
-        if number == 4:
-            spot = out.at[row_of(p)]
-            flying[p] = [send(spot, spot, p, again + first_t + i, device) for i, device in enumerate(sides)]
-        if number == 5:
-            spot = out.at[half_of(p, core)]
-            flying[p] = [send(spot, spot, p, again, twin)]
-
-    for number in (0, 1):
-        for p in range(PIECES):
-            stage(p, number)
-    for tick in range(2, 5 + PIECES + 2):
-        for p in range(PIECES):
-            number = tick - p
-            if 2 <= number <= 6:
-                stage(p, number)
-    for copy in sent:
-        copy.wait_send()
+    for copy in copies:
+        copy.wait()
 
 
 def vmem(count):
@@ -669,7 +775,7 @@
 
 
 SMEM_SPEC = pl.BlockSpec(memory_space=pltpu.SMEM)
-LIMIT = 60 * 1024 * 1024
+LIMIT = 50 * 1024 * 1024
 
 
 def shape(dims, dtype=F32):
@@ -681,18 +787,29 @@
     hid = w_in.shape[0]
     pops, cot = (v.reshape(Q * cells // LANES, LANES) for v in (populations, cotangent))
     w_mid = w_mid[0]
-    step = 8 * blocks * PIECES
-    total_rows = -(-(hid + 2 * R) // step) * step
+    pieces = piece_rows(blocks, hid)
+    rows, most = 2 * sum(pieces), max(pieces)
+    sizes = [part_size(n, blocks, hid) for n in pieces]
+    small = tuple(max(size[axis] for size in sizes) for axis in range(2))
+    pieces = len(pieces)
     volume = pltpu.VMEM((ROWS, LANES), F32)
     thin = pltpu.VMEM((R, cells), BF16)
     deep = pltpu.VMEM((hid, cells), BF16)
     slots = 2 * REACH + 3
-    final, grad_pops, grads = pl.pallas_call(
+    final, grad_pops, total = pl.pallas_call(
         functools.partial(step_kernel, blocks, slabs),
-        out_shape=(shape(pops.shape), shape(pops.shape), shape((total_rows, hid))),
-        in_specs=[SMEM_SPEC] * 3 + vmem(5),
+        out_shape=(shape(pops.shape), shape(pops.shape), shape((rows, hid))),
+        in_specs=[SMEM_SPEC] * 3 + [pl.BlockSpec(memory_space=pltpu.HBM)] * 5,
         out_specs=tuple(vmem(3)),
-        scratch_shapes=[volume] * 4 + [thin] * 3 + [deep] * 6 + [
+        scratch_shapes=[
+            pltpu.VMEM((rows, hid), F32),
+            pltpu.VMEM((pieces, most, hid), F32),
+            pltpu.VMEM((pieces, most, hid), F32),
+            pltpu.VMEM((pieces, blocks - 1, *small), F32),
+            pltpu.VMEM((pieces, *small), F32),
+            pltpu.VMEM((pieces, max(slabs // 2 - 1, 1), *small), F32),
+            pltpu.SemaphoreType.DMA((2, pieces, 2 * blocks + slabs // 2 + 1)),
+        ] + [volume] * 4 + [thin] * 3 + [deep] * 6 + [pltpu.VMEM((hid, cells), F32)] + [
             *[pltpu.VMEM((3, SHEET_ROWS, LANES), F32)] * 4,
             *[pltpu.VMEM((slots, SHEET_ROWS, LANES), F32)] * 4,
             pltpu.VMEM((3, SHEET_ROWS, LANES), F32),
@@ -705,36 +822,37 @@
             pltpu.VMEM((hid, R), BF16),
             pltpu.VMEM((hid, hid), BF16),
             pltpu.VMEM((R, hid), F32),
+            pltpu.VMEM(pops.shape, F32),
+            pltpu.VMEM(cot.shape, F32),
+            pltpu.VMEM((Q, hid), BF16),
+            pltpu.VMEM((hid, hid), BF16),
+            pltpu.VMEM((Q, hid), BF16),
+            pltpu.SemaphoreType.DMA((5,)),
             pltpu.SemaphoreType.DMA((4, 2, slots)),
         ],
         compiler_params=pltpu.CompilerParams(vmem_limit_bytes=LIMIT, collective_id=0, has_side_effects=True),
         name="step",
-    )(face_source.T, face_level, face_quadrant, pops, cot, w_in.T, w_mid, w_out)
-    chips = blocks // 2
-    rows, width = total_rows // (blocks * PIECES), hid // slabs
-    total = pl.pallas_call(
-        functools.partial(sum_kernel, chips, slabs),
-        out_shape=shape((total_rows, hid)),
-        in_specs=vmem(1),
-        out_specs=vmem(1)[0],
-        scratch_shapes=[
-            pltpu.VMEM((PIECES, chips * rows, hid), F32),
-            pltpu.VMEM((PIECES, chips * rows, hid), F32),
-            pltpu.VMEM((PIECES, chips - 1, rows, hid), F32),
-            pltpu.VMEM((PIECES, rows, hid), F32),
-            pltpu.VMEM((PIECES, slabs - 1, rows, width), F32),
-            pltpu.SemaphoreType.DMA((2, PIECES, 2 * (chips + slabs - 1))),
-        ],
-        compiler_params=pltpu.CompilerParams(collective_id=2, has_side_effects=True),
-        name="sum_all",
-    )(grads)
-    total = total * float(blocks * slabs * cells) ** (-0.5)
+    )(*[
+        pltpu.with_memory_space_constraint(v, pltpu.HBM)
+        for v in (face_source.T, face_level, face_quadrant, pops, cot, w_in.T, w_mid, w_out)
+    ])
+    final, grad_pops, grad_mid, grad_in, grad_out = pl.pallas_call(
+        leave_kernel,
+        out_shape=(
+            shape(pops.shape), shape(pops.shape), shape((hid, hid)), shape((Q, hid)), shape((Q, hid)),
+        ),
+        in_specs=vmem(3),
+        out_specs=tuple([pl.BlockSpec(memory_space=pl.ANY)] * 5),
+        scratch_shapes=[pltpu.VMEM((Q, hid), F32), pltpu.VMEM((Q, hid), F32), pltpu.SemaphoreType.DMA((5,))],
+        compiler_params=pltpu.CompilerParams(vmem_limit_bytes=4 * 1024 * 1024),
+        name="leave",
+    )(final, grad_pops, total)
     return (
         final.reshape(populations.shape),
         grad_pops.reshape(populations.shape),
-        total[hid : hid + Q].T,
-        total[:hid][None],
-        total[hid + R : hid + R + Q],
+        grad_in.T,
+        grad_mid[None],
+        grad_out,
     )
 
 

time: 78.7 us -> 62.1 us (0.79)
  Pallas kernels: 73.3 us -> 61.2 us
  local copies, waits for them, and re-layouts: 3.13 us -> 0 us
  other arithmetic: 1.4 us -> 0 us
    pallas_call x1, Pallas kernels: 30.8 us -> 1.23 us  [shards(): pl.pallas_call(leave_kernel, out_shape=(shape(pops.shape), shape(pops.sha...]
    pallas_call x1, Pallas kernels: 42.5 us -> 59.9 us  [shards(): pl.pallas_call(functools.partial(step_kernel, blocks, slabs), out_shape=(...]
    unnamed x6 -> x0, local copies, waits for them, and re-layouts: 1.45 us -> none
    mul x1 -> x0, other arithmetic: 1.4 us -> none  [shards(): total = total * float(blocks * slabs * cells) ** (-0.5)]
    broadcast_in_dim x1 -> x0, local copies, waits for them, and re-layouts: 1.04 us -> none  [shards(): total[:hid][None]]
where the time goes in v2:
time: 62.1 us; the launch traced here: 62 us
  Pallas kernels  61.2 us (99%)
  between operations  0.8 us (1%)
    pallas_call x1, Pallas kernels, shards(): pl.pallas_call(functools.partial(step_kernel, blocks, slabs), out_shape=(...  59.9 us

profile of v2, /device:TPU:0, one launch (start us, length us, event | category | flops | bytes accessed | tf_op | source)
XLA Modules:
  0.0 62.0 jit_solution(1611908994747358259)
XLA Ops:
  0.6 59.9 %step.1 = (f32[608,128]{1,0:T(8,128)S(1)}, f32[608,128]{1,0:T(8,128)S(1)}, f32[576,512]{1,0:T(8,128)S(1)}) custom-call(s32[4,8]{1,0:T(4,128)} %bitcast.13, s32[1,1,6]{2,1,0:T(1,128)} %level.1, s32[1,1,6]{2,1,0:T(1,128)} %quadrant.1, f32[608,128]{1,0:T(8,128)} %bitcast.10, f32[608,128]{1,0:T(8,128)} %bitcast.11, bf16[19,512]{1,0:T(8,128)(2,1)} %bitcast.12, ...), custom_call_target="tpu_custom_call" | custom-call | tf_op jit(solution)/shard_map/step/pallas_call | solution.py:799
  60.6 1.2 %leave.1 = (f32[608,128]{1,0:T(8,128)}, f32[608,128]{1,0:T(8,128)}, f32[512,512]{1,0:T(8,128)}, f32[19,512]{1,0:T(8,128)}, f32[19,512]{1,0:T(8,128)}) custom-call(f32[608,128]{1,0:T(8,128)S(1)} %get-tuple-element.13.final, f32[608,128]{1,0:T(8,128)S(1)} %get-tuple-element.14.grad_pops, f32[576,512]{1,0:T(8,128)S(1)} %get-tuple-element.15.total), custom_call_target="tpu_custom_call" | custom-call | tf_op jit(solution)/shard_map/leave/pallas_call | solution.py:839

commit v3 on v2

--- a/solution.py
+++ b/solution.py
@@ -435,22 +435,21 @@
     flipped[...] = tall[...].T.astype(BF16)
 
 
-BIG = 4
+BIG = 2
 STAGES = 6
+DIRECT = True
 
 
 class Total:
-    def __init__(self, blocks, slabs, hid, grads, out, land_c, half, land_a, tile, land_z, sems, scale):
+    def __init__(self, blocks, slabs, hid, grads, out, land_c, half, land_a, land_all, tile, land_z, sems, scale):
         self.me, self.level = lax.axis_index("blocks"), lax.axis_index("slab")
-        self.chips, self.pairs, self.scale = blocks // 2, slabs // 2, scale
-        self.count = self.chips * 2
+        self.chips, self.slabs, self.pairs, self.scale = blocks // 2, slabs, slabs // 2, scale
         self.core, self.chip = lax.rem(self.me, 2), self.me // 2
         self.low, self.high = lax.rem(self.level, 2), self.level // 2
-        self.at = self.chip * 2 + self.low
         self.grads, self.out, self.land_c, self.half = grads, out, land_c, half
-        self.land_a, self.tile, self.land_z, self.sems = land_a, tile, land_z, sems
+        self.land_a, self.land_all, self.tile, self.land_z, self.sems = land_a, land_all, tile, land_z, sems
         self.hid = hid
-        self.rows = piece_rows(blocks, hid)
+        self.rows = piece_rows(blocks, slabs, hid)
         self.first = [sum(2 * n for n in self.rows[:p]) for p in range(len(self.rows))]
         self.flying = [[] for _ in self.rows]
         self.done = []
@@ -474,7 +473,7 @@
         return pl.ds(pl.multiple_of(self.first[p] + core * n, 8), n)
 
     def size(self, p):
-        return part_size(self.rows[p], self.count, self.hid)
+        return part_size(self.rows[p], self.chips * self.spread(p), self.hid)
 
     def part(self, p, t, start):
         n, w = self.size(p)
@@ -485,57 +484,79 @@
     def twin(self):
         return {"blocks": self.me + 1 - 2 * self.core}
 
-    def near(self):
-        for d in range(1, self.count):
-            t = lax.rem(self.at + d, self.count)
-            yield d - 1, t, {"blocks": t // 2 * 2 + self.core, "slab": self.high * 2 + lax.rem(t, 2)}
+    def spread(self, p):
+        return self.slabs if self.direct(p) else 2
+
+    def direct(self, p):
+        return DIRECT and p == BIG
+
+    def at(self, p):
+        return self.chip * self.spread(p) + (self.level if self.direct(p) else self.low)
+
+    def near(self, p):
+        spread, base = self.spread(p), 0 if self.direct(p) else self.high * 2
+        count = self.chips * spread
+        for d in range(1, count):
+            t = lax.rem(self.at(p) + d, count)
+            yield d - 1, t, {"blocks": t // spread * 2 + self.core, "slab": base + lax.rem(t, spread)}
 
     def far(self):
         for d in range(1, self.pairs):
             yield d - 1, {"slab": lax.rem(self.high + d, self.pairs) * 2 + self.low}
 
     def friends(self):
-        return [device for _, _, device in self.near()] + [device for _, device in self.far()]
+        return [device for _, _, device in self.near(BIG)] + ([] if DIRECT else [device for _, device in self.far()])
 
     def stage(self, p, number):
         n, w = self.size(p)
         whole, small = pl.ds(0, self.rows[p]), (pl.ds(0, n), pl.ds(0, w))
-        tile = self.tile.at[p, *small]
-        again = self.count + self.pairs
+        land = self.land_all if p == BIG else self.land_a.at[p]
+        count = self.chips * self.spread(p)
+        again = count + self.pairs
         start = self.first[p] + self.core * self.rows[p]
         self.settle(p)
+
+        def gathered():
+            total = self.half[p, *self.part(p, self.at(p), 0)]
+            for i in range(count - 1):
+                total += land[i, *small]
+            return total
+
+        def hand_out(total):
+            spot = self.out.at[*self.part(p, self.at(p), start)]
+            spot[...] = total * self.scale
+            for i, t, device in self.near(p):
+                self.go(p, spot, spot, again + i, device)
+
         if number == 0:
             self.go(p, self.grads.at[self.rows_of(p, 1 - self.core)], self.land_c.at[p, whole], 0, self.twin())
         elif number == 1:
             self.half[p, whole] = self.grads[self.rows_of(p, self.core)] + self.land_c[p, whole]
-            for i, t, device in self.near():
-                self.go(p, self.half.at[p, *self.part(p, t, 0)], self.land_a.at[p, i, *small], 1 + i, device)
+            for i, t, device in self.near(p):
+                self.go(p, self.half.at[p, *self.part(p, t, 0)], land.at[i, *small], 1 + i, device)
+        elif number == 2 and self.direct(p):
+            hand_out(gathered())
         elif number == 2:
-            total = self.half[p, *self.part(p, self.at, 0)]
-            for i in range(self.count - 1):
-                total += self.land_a[p, i, *small]
-            tile[...] = total
+            tile = self.tile.at[p, *small]
+            tile[...] = gathered()
             for i, device in self.far():
-                self.go(p, tile, self.land_z.at[p, i, *small], self.count + i, device)
-        elif number == 3:
-            total = tile[...]
+                self.go(p, tile, self.land_z.at[p, i, *small], count + i, device)
+        elif number == 3 and not self.direct(p):
+            total = self.tile[p, *small]
             for i in range(self.pairs - 1):
                 total += self.land_z[p, i, *small]
-            spot = self.out.at[*self.part(p, self.at, start)]
-            spot[...] = total * self.scale
-            for i, t, device in self.near():
-                self.go(p, spot, spot, again + i, device)
-        elif number == 4:
+            hand_out(total)
+        elif number == STAGES - 2 - self.direct(p):
             rows = self.out.at[self.rows_of(p, self.core)]
-            self.go(p, rows, rows, again + self.count, self.twin())
+            self.go(p, rows, rows, again + count, self.twin())
 
     def close(self):
         for copy in self.done:
             copy.wait_send()
 
 
-def piece_rows(blocks, hid):
-    return [hid // BIG // 2] * BIG + [max(R + 8, blocks * 8 * LANES // hid)]
+def piece_rows(blocks, slabs, hid):
+    return [hid // BIG // 2] * BIG + [max(R + 8, blocks // 2 * slabs * 8 * LANES // hid)]
 
 
 def part_size(rows, count, hid):
@@ -591,7 +612,7 @@
 def step_kernel(
     blocks, slabs, source, level, quadrant, pops_hbm, cot_hbm, w_in_hbm, w_mid_hbm, w_out_hbm,
     final, grad_pops, out,
-    grads, land_c, half_c, land_a, tile, land_z, total_sems, fa, fb, ca, cb, x1, x2, e, h0a, h1a, h0b, h1b, a1, a0, u,
+    grads, land_c, half_c, land_a, land_all, tile, land_z, total_sems, fa, fb, ca, cb, x1, x2, e, e2, h0a, h1a, h0b, h1b, a1, a0, u,
     sheets0, sheets1, sheets2, sheets3, recv0, recv1, recv2, recv3, tmp, ghosts, shifted, picks, w_in, w_in_t, w_out, w_out_t, w_mid_t, tall,
     pops, cot, w_in_rows, w_mid, w_out_rows, load_sems, sems,
 ):
@@ -611,7 +632,7 @@
         ref[:, SHEET:, :] = jnp.zeros((ref.shape[0], SHEET_ROWS - SHEET, LANES), F32)
     link = Exchange(blocks, slabs)
     total = Total(
-        blocks, slabs, hid, grads, out, land_c, half_c, land_a, tile, land_z, total_sems,
+        blocks, slabs, hid, grads, out, land_c, half_c, land_a, land_all, tile, land_z, total_sems,
         float(blocks * slabs * cells) ** (-0.5),
     )
     link.friends = total.friends()
@@ -635,7 +656,7 @@
     padded_rows(w_out_rows, tall, w_out, w_out_t)
     from_cells(fa, pops)
 
-    def forward(f, x, h0, h1):
+    def forward(f, x, h0, h1, lifted):
         @pl.loop(0, chunks)
         def _(i):
             at = span(i)
@@ -646,25 +667,24 @@
             h0[:, at] = first
             second = jnp.tanh(mm(w_mid[...], first)).astype(BF16)
             h1[:, at] = second
+            if lifted:
+                a1[:, at] = damp(u[:, at], second)
             put_lines(f, i, state + mm(w_out[...], second))
 
-    def backward(p, h0, h1):
+    def backward(p, h0):
         @pl.loop(0, chunks)
         def _(i):
             at = span(i)
-            bar = get_lines(p, i)
-            second = damp(u[:, at], h1[:, at])
-            a1[:, at] = second
-            first = damp(mm(w_mid_t[...], second), h0[:, at])
+            first = damp(mm(w_mid_t[...], a1[:, at]), h0[:, at])
             a0[:, at] = first
-            put_lines(p, i, bar + mm(w_in_t[...], first))
+            put_lines(p, i, get_lines(p, i) + mm(w_in_t[...], first))
 
     def lift(p):
         @pl.loop(0, chunks)
         def _(i):
             at = span(i)
             err = get_lines(p, i).astype(BF16)
-            e[:, at] = err
+            e2[:, at] = err
             u[:, at] = mm(w_out_t[...], err)
 
     def top_down(h1, first, count):
@@ -687,7 +707,7 @@
         at = (spot_rows, columns or slice(None))
         grads[at] = grads[at] + value if old else value
 
-    forward(fa, x1, h0a, h1a)
+    forward(fa, x1, h0a, h1a, False)
     gather_sheets(g, fa, sheets1)
     posts1 = link.send(sheets1, recv1, sems.at[1])
     w_mid_t[...] = w_mid[...].astype(F32).T.astype(BF16)
@@ -699,10 +719,10 @@
     settle(recv1, slots, picks, fa, ghosts)
     stream(g, fa, ghosts, shifted, functools.partial(save, fb))
 
-    forward(fb, x2, h0b, h1b)
+    forward(fb, x2, h0b, h1b, True)
     gather_sheets(g, fb, sheets2)
     posts2 = link.send(sheets2, recv2, sems.at[2])
-    backward(cb, h0b, h1b)
+    backward(cb, h0b)
     send_bars(g, cb, tmp, sheets3, picks)
     bars1 = link.send(sheets3, recv3, sems.at[3])
     mid = hid // 2
@@ -710,7 +730,6 @@
     weigh(0, a1.at[:mid], h0b, False)
     weigh(mid, a1.at[mid:], h0b, False)
     weigh(hid, x2, a0, False)
-    weigh(second, e, h1b, False)
     arrive(posts2)
     settle(recv2, slots, picks, fb, ghosts)
     stream(g, fb, ghosts, shifted, functools.partial(to_cells, final))
@@ -724,27 +743,41 @@
         for p, number in pairs:
             total.stage(p, number)
 
+    low, high = range(BIG // 2), range(BIG // 2, BIG)
+
+    def turn(number, *groups):
+        for group in groups:
+            for p in group:
+                total.stage(p, number)
+
     top_down(h1a, 0, mid)
     weigh(0, a1.at[:mid], h0a, True)
-    turns((0, 0), (1, 0))
+    turn(0, low)
     top_down(h1a, mid, mid)
     weigh(mid, a1.at[mid:], h0a.at[:mid], True, slice(0, mid))
-    turns((0, 1), (1, 1))
+    turn(1, low)
     weigh(mid, a1.at[mid:], h0a.at[mid:], True, slice(mid, hid))
-    turns((2, 0), (3, 0))
+    turn(0, high)
+    weigh(second, e2, h1b, False)
+    turn(1, high)
     weigh(second, e, h1a, True)
-    turns((2, 1), (3, 1))
     for i in range(chunks):
         bottom(fa, h0a, i)
+    turn(2, low)
     weigh(hid, x1, a0, True)
-    turns((BIG, 0))
+    turn(0, [BIG])
+    turn(2, high)
+    turn(1, [BIG])
     for q in range(Q):
         for half in range(HALVES):
             to_cells(grad_pops, q, half, load(fa, q, half))
-    turns((0, 2), (1, 2), (BIG, 1), (2, 2), (3, 2))
-    for number in range(3, STAGES):
-        turns((0, number), (1, number), (2, number), (3, number), (BIG, number - 1))
-    turns((BIG, STAGES - 1))
+    turn(3, low, high)
+    turn(2, [BIG])
+    turn(4, low)
+    turn(3, [BIG])
+    turn(4, high)
+    turn(4, [BIG])
+    turn(5, low, high, [BIG])
     total.close()
     for copies in (bars2, posts1, posts2, bars1):
         for copy in copies:
@@ -787,10 +820,9 @@
     hid = w_in.shape[0]
     pops, cot = (v.reshape(Q * cells // LANES, LANES) for v in (populations, cotangent))
     w_mid = w_mid[0]
-    pieces = piece_rows(blocks, hid)
+    pieces = piece_rows(blocks, slabs, hid)
     rows, most = 2 * sum(pieces), max(pieces)
-    sizes = [part_size(n, blocks, hid) for n in pieces]
-    small = tuple(max(size[axis] for size in sizes) for axis in range(2))
+    small, last = part_size(pieces[0], blocks, hid), part_size(pieces[-1], blocks // 2 * (slabs if DIRECT else 2), hid)
     pieces = len(pieces)
     volume = pltpu.VMEM((ROWS, LANES), F32)
     thin = pltpu.VMEM((R, cells), BF16)
@@ -805,11 +837,12 @@
             pltpu.VMEM((rows, hid), F32),
             pltpu.VMEM((pieces, most, hid), F32),
             pltpu.VMEM((pieces, most, hid), F32),
-            pltpu.VMEM((pieces, blocks - 1, *small), F32),
+            pltpu.VMEM((BIG, blocks - 1, *small), F32),
+            pltpu.VMEM((blocks // 2 * (slabs if DIRECT else 2) - 1, *last), F32),
             pltpu.VMEM((pieces, *small), F32),
             pltpu.VMEM((pieces, max(slabs // 2 - 1, 1), *small), F32),
-            pltpu.SemaphoreType.DMA((2, pieces, 2 * blocks + slabs // 2 + 1)),
-        ] + [volume] * 4 + [thin] * 3 + [deep] * 6 + [pltpu.VMEM((hid, cells), F32)] + [
+            pltpu.SemaphoreType.DMA((2, pieces, blocks * slabs + slabs // 2 + 1)),
+        ] + [volume] * 4 + [thin] * 4 + [deep] * 6 + [pltpu.VMEM((hid, cells), F32)] + [
             *[pltpu.VMEM((3, SHEET_ROWS, LANES), F32)] * 4,
             *[pltpu.VMEM((slots, SHEET_ROWS, LANES), F32)] * 4,
             pltpu.VMEM((3, SHEET_ROWS, LANES), F32),

time: 62.1 us -> 61.5 us (level)
  Pallas kernels: 61.2 us -> 60.5 us
where the time goes in v3:
time: 61.5 us; the launch traced here: 61.4 us
  Pallas kernels  60.5 us (98%)
  between operations  0.8 us (1%)
    pallas_call x1, Pallas kernels, shards(): pl.pallas_call(functools.partial(step_kernel, blocks, slabs), out_shape=(...  59.3 us
    pallas_call x1, Pallas kernels, shards(): pl.pallas_call(leave_kernel, out_shape=(shape(pops.shape), shape(pops.sha...  1.23 us

profile of v3, /device:TPU:0, one launch (start us, length us, event | category | flops | bytes accessed | tf_op | source)
XLA Modules:
  0.0 61.4 jit_solution(17396027405376048826)
XLA Ops:
  0.6 59.3 %step.1 = (f32[608,128]{1,0:T(8,128)S(1)}, f32[608,128]{1,0:T(8,128)S(1)}, f32[576,512]{1,0:T(8,128)S(1)}) custom-call(s32[4,8]{1,0:T(4,128)} %bitcast.13, s32[1,1,6]{2,1,0:T(1,128)} %level.1, s32[1,1,6]{2,1,0:T(1,128)} %quadrant.1, f32[608,128]{1,0:T(8,128)} %bitcast.10, f32[608,128]{1,0:T(8,128)} %bitcast.11, bf16[19,512]{1,0:T(8,128)(2,1)} %bitcast.12, ...), custom_call_target="tpu_custom_call" | custom-call | tf_op jit(solution)/shard_map/step/pallas_call | solution.py:831
  60.0 1.2 %leave.1 = (f32[608,128]{1,0:T(8,128)}, f32[608,128]{1,0:T(8,128)}, f32[512,512]{1,0:T(8,128)}, f32[19,512]{1,0:T(8,128)}, f32[19,512]{1,0:T(8,128)}) custom-call(f32[608,128]{1,0:T(8,128)S(1)} %get-tuple-element.13.final, f32[608,128]{1,0:T(8,128)S(1)} %get-tuple-element.14.grad_pops, f32[576,512]{1,0:T(8,128)S(1)} %get-tuple-element.15.total), custom_call_target="tpu_custom_call" | custom-call | tf_op jit(solution)/shard_map/leave/pallas_call | solution.py:872

commit v4 on v3

--- a/solution.py
+++ b/solution.py
@@ -672,17 +672,15 @@
             put_lines(f, i, state + mm(w_out[...], second))
 
     def backward(p, h0):
-        @pl.loop(0, chunks)
-        def _(i):
-            at = span(i)
+        for i in range(chunks):
+            at = pl.ds(i * CHUNK, CHUNK)
             first = damp(mm(w_mid_t[...], a1[:, at]), h0[:, at])
             a0[:, at] = first
             put_lines(p, i, get_lines(p, i) + mm(w_in_t[...], first))
 
     def lift(p):
-        @pl.loop(0, chunks)
-        def _(i):
-            at = span(i)
+        for i in range(chunks):
+            at = pl.ds(i * CHUNK, CHUNK)
             err = get_lines(p, i).astype(BF16)
             e2[:, at] = err
             u[:, at] = mm(w_out_t[...], err)
@@ -690,9 +688,8 @@
     def top_down(h1, first, count):
         rows = pl.ds(first, count)
 
-        @pl.loop(0, chunks)
-        def _(i):
-            at = span(i)
+        for i in range(chunks):
+            at = pl.ds(i * CHUNK, CHUNK)
             a1[rows, at] = damp(mm(w_out_t[rows], e[:, at]), h1[rows, at])
 
     def bottom(p, h0, i):

time: 61.5 us -> 60 us (0.976)
  Pallas kernels: 60.5 us -> 59 us
    pallas_call x1, Pallas kernels: 59.3 us -> 57.7 us  [shards(): pl.pallas_call(functools.partial(step_kernel, blocks, slabs), out_shape=(...]
where the time goes in v4:
time: 60 us; the launch traced here: 59.8 us
  Pallas kernels  59 us (98%)
  between operations  0.82 us (1%)
    pallas_call x1, Pallas kernels, shards(): pl.pallas_call(functools.partial(step_kernel, blocks, slabs), out_shape=(...  57.7 us
    pallas_call x1, Pallas kernels, shards(): pl.pallas_call(leave_kernel, out_shape=(shape(pops.shape), shape(pops.sha...  1.23 us

profile of v4, /device:TPU:0, one launch (start us, length us, event | category | flops | bytes accessed | tf_op | source)
XLA Modules:
  0.0 59.8 jit_solution(13007799191569894724)
XLA Ops:
  0.6 57.7 %step.1 = (f32[608,128]{1,0:T(8,128)S(1)}, f32[608,128]{1,0:T(8,128)S(1)}, f32[576,512]{1,0:T(8,128)S(1)}) custom-call(s32[4,8]{1,0:T(4,128)} %bitcast.13, s32[1,1,6]{2,1,0:T(1,128)} %level.1, s32[1,1,6]{2,1,0:T(1,128)} %quadrant.1, f32[608,128]{1,0:T(8,128)} %bitcast.10, f32[608,128]{1,0:T(8,128)} %bitcast.11, bf16[19,512]{1,0:T(8,128)(2,1)} %bitcast.12, ...), custom_call_target="tpu_custom_call" | custom-call | tf_op jit(solution)/shard_map/step/pallas_call | solution.py:828
  58.4 1.2 %leave.1 = (f32[608,128]{1,0:T(8,128)}, f32[608,128]{1,0:T(8,128)}, f32[512,512]{1,0:T(8,128)}, f32[19,512]{1,0:T(8,128)}, f32[19,512]{1,0:T(8,128)}) custom-call(f32[608,128]{1,0:T(8,128)S(1)} %get-tuple-element.13.final, f32[608,128]{1,0:T(8,128)S(1)} %get-tuple-element.14.grad_pops, f32[576,512]{1,0:T(8,128)S(1)} %get-tuple-element.15.total), custom_call_target="tpu_custom_call" | custom-call | tf_op jit(solution)/shard_map/leave/pallas_call | solution.py:869
